TPU v7x, 256 devices: a whole 4x4x8 slice. The times are simulated.
256 devices in a mesh: gz: 8 (over z), gy: 8 (over x, core), gx: 4 (over y).
Axes of the slice: x: 4, y: 4, z: 8, core: 2. Of those that a mesh axis runs over, the one named last changes fastest.
Arguments:
- fields: float32 [5, 256, 128, 512], P(None, 'gz', 'gy', 'gx'), may hold values from -6 to 6
- diffusivity: float32 [256, 128, 512], P('gz', 'gy', 'gx'), may hold values from 0.01 to 0.08
- courant: float32 [5, 3], replicated, may hold values from 0.03 to 0.1
- tf_center: float32 [16], replicated, may hold values from -1.5 to 1.5
- tf_sharp: float32 [16], replicated, may hold values from 0.5 to 4
- tf_gain: float32 [16], replicated, may hold values from 0.01 to 0.12
- tf_color: float32 [3, 16], replicated, may hold values from 0.2 to 1
- tile_mask: int32 [8, 16, 128, 4], P('gz', None, 'gy', 'gx'), may hold values from 0 to 1, as said below
- tile_perm: int32 [8, 4, 256], P('gy', 'gx'), may hold values from 0 to 255, each once within a row
Outputs:
- advanced: float32 [5, 256, 128, 512], P(None, 'gz', 'gy', 'gx')
- picture: float32 [8, 4, 256, 4, 128], P('gy', 'gx', 'gz')
Inputs may be any that keep to these rules, and one draw needn't show every extreme that they name: `tile_mask`: 1 marks an active tile; the share of active tiles differs from slab to slab.
All inputs are finite; a program needn't handle non-finite values.
Results may differ from a plain program's by a relative error of at most 0.0001.
Values sent between devices are 32-bit elements; how exact they have to be, the bound alone decides.
A program may use at most 64 MiB of HBM per device.

v0:
```python
import jax
import jax.numpy as jnp
from jax import lax
from jax.sharding import PartitionSpec as P


def extended(cells, sides, width):
    for axis, dim in sides:
        count = lax.axis_size(axis)
        ends = count - 1
        head = lax.slice_in_dim(cells, 0, width, axis=dim)
        tail = lax.slice_in_dim(cells, cells.shape[dim] - width, cells.shape[dim], axis=dim)
        cells = jnp.concatenate(
            [
                lax.ppermute(tail, axis, [(i, (i + 1) % count) for i in range(ends)]),
                cells,
                lax.ppermute(head, axis, [((i + 1) % count, i) for i in range(ends)]),
            ],
            axis=dim,
        )
    return cells


def inner(source, leading, axis_pos, offset):
    picks = [slice(None)] * leading + [slice(1, -1)] * 3
    length = source.shape[leading + axis_pos]
    picks[leading + axis_pos] = slice(1 + offset, length - 1 + offset)
    return source[tuple(picks)]


def advance(padded, kappa_pad, courant):
    center = inner(padded, 1, 0, 0)
    kappa_mid = inner(kappa_pad, 0, 0, 0)
    result = center
    for axis_pos in range(3):
        upper = inner(padded, 1, axis_pos, 1)
        lower = inner(padded, 1, axis_pos, -1)
        kappa_up = inner(kappa_pad, 0, axis_pos, 1)
        kappa_down = inner(kappa_pad, 0, axis_pos, -1)
        speed = courant[:, axis_pos][:, None, None, None]
        result = (
            result
            + 0.5 * (kappa_mid + kappa_up) * (upper - center)
            + 0.5 * (kappa_mid + kappa_down) * (lower - center)
            - speed * (center - lower)
        )
    return result


def over(front, back):
    front_alpha = front[:, 3:4]
    color = front[:, :3] + (1.0 - front_alpha) * back[:, :3]
    alpha = front_alpha + (1.0 - front_alpha) * back[:, 3:4]
    return jnp.concatenate([color, alpha], 1)


def fold_slabs(received):
    result = received[0]
    for slab in range(1, received.shape[0]):
        result = over(result, received[slab])
    return result


def shards(
    fields, diffusivity, courant, tf_center, tf_sharp, tf_gain, tf_color, tile_mask, tile_perm
):
    nfield, depth_len, rows_len, cols_len = fields.shape
    stacked = jnp.concatenate([fields, diffusivity[None]], 0)
    padded = extended(stacked, (("gz", 1), ("gy", 2), ("gx", 3)), 1)
    kappa_pad = padded[nfield]
    once = advance(padded[:nfield], kappa_pad, courant)
    again = extended(once, (("gz", 1), ("gy", 2), ("gx", 3)), 1)
    state = advance(again, kappa_pad, courant)
    scalar = state[0]
    spad = extended(scalar, (("gz", 0), ("gy", 1), ("gx", 2)), 1)
    grad_z = 0.5 * (spad[2:, 1:-1, 1:-1] - spad[:-2, 1:-1, 1:-1])
    grad_y = 0.5 * (spad[1:-1, 2:, 1:-1] - spad[1:-1, :-2, 1:-1])
    grad_x = 0.5 * (spad[1:-1, 1:-1, 2:] - spad[1:-1, 1:-1, :-2])
    shade = 0.35 + 0.65 * jnp.abs(0.64 * grad_z + 0.6 * grad_y + 0.48 * grad_x) / jnp.sqrt(
        grad_z * grad_z + grad_y * grad_y + grad_x * grad_x + 1.0
    )
    modul = 1.0 + 0.5 * jnp.tanh(state[4])
    bases = shade[None] * jax.nn.sigmoid(state[1:4])
    steps_idx = jnp.arange(depth_len, dtype=jnp.int32)
    earlier = (steps_idx[:, None] > steps_idx[None, :]).astype(jnp.float32)

    def render(items):
        center, sharp, gain, color = items
        depth = gain * jnp.exp(-sharp * (scalar - center) ** 2) * modul
        before = jnp.einsum("wz,zyx->wyx", earlier, depth, precision=lax.Precision.HIGHEST)
        weight = jnp.exp(-before) * (1.0 - jnp.exp(-depth))
        colors = jnp.sum(weight[None] * bases, axis=1) * color[:, None, None]
        alpha = 1.0 - jnp.exp(-jnp.sum(depth, axis=0))
        return jnp.transpose(jnp.concatenate([colors, alpha[None]], 0), (1, 0, 2))

    rendered = lax.map(render, (tf_center, tf_sharp, tf_gain, tf_color.T))
    cover = tile_mask[0].astype(jnp.float32)[..., None]
    tiles = (rendered * cover).reshape(-1, 4, cols_len)
    order = tile_perm[0, 0]
    count = lax.axis_size("gz")
    per_owner = tiles.shape[0] // count
    grouped = tiles[order].reshape(count, per_owner, 4, cols_len)
    composed = fold_slabs(lax.all_to_all(grouped, "gz", split_axis=0, concat_axis=0, tiled=True))
    picture = composed.reshape(1, 1, per_owner, 4, cols_len)
    return (state, picture)


def solution(mesh):
    return jax.shard_map(
        shards,
        mesh=mesh,
        in_specs=(
            P(None, "gz", "gy", "gx"),
            P("gz", "gy", "gx"),
            P(),
            P(),
            P(),
            P(),
            P(),
            P("gz", None, "gy", "gx"),
            P("gy", "gx", None),
        ),
        out_specs=(P(None, "gz", "gy", "gx"), P("gy", "gx", "gz", None, None)),
        check_vma=False,
    )
```

profile of v0, /device:TPU:26, one launch (start us, length us, event | category | flops | bytes accessed | tf_op | source)
XLA Modules:
  0.0 247.0 jit_solution(12370888466228039329)
XLA Ops:
  1.6 3.8 %collective-permute-start = (f32[6,1,16,128]{3,2,1,0:T(8,128)S(1)}, f32[6,1,16,128]{3,2,1,0:T(8,128)S(1)}, u32[]{:S(2)}, u32[]{:S(2)}) collective-permute-start(f32[6,1,16,128]{3,2,1,0:T(8,128)S(1)} %get-tuple-element.158), channel_id=1, source_target_pairs={{0,32},{32,64},{64,96},{96,128},{128,160},{160,192},{192,224},{1,3... | collective-permute-start | bytes 147464 | tf_op jit(solution)/shard_map/ppermute | solution.py:15
  7.2 4.2 %collective-permute-done.1 = f32[6,1,16,128]{3,2,1,0:T(8,128)S(1)} collective-permute-done((f32[6,1,16,128]{3,2,1,0:T(8,128)S(1)}, f32[6,1,16,128]{3,2,1,0:T(8,128)S(1)}, u32[]{:S(2)}, u32[]{:S(2)}) %collective-permute-start.1) | collective-permute-done | bytes 49184 | tf_op jit(solution)/shard_map/ppermute | solution.py:17
  13.5 3.6 %collective-permute-start.3 = (f32[6,34,1,128]{3,2,1,0:T(1,128)S(1)}, f32[6,34,1,128]{3,2,1,0:T(1,128)S(1)}, u32[]{:S(2)}, u32[]{:S(2)}) collective-permute-start(f32[6,34,1,128]{3,2,1,0:T(1,128)S(1)} %get-tuple-element.157), channel_id=1, source_target_pairs={{4,0},{8,4},{12,8},{16,12},{20,16},{24,20},{28,24},{5,1},{9,5},{13... | collective-permute-start | bytes 313352 | tf_op jit(solution)/shard_map/ppermute | solution.py:17
  19.8 3.0 %fusion.100 = (f32[6,34,18,1]{3,2,1,0:T(8,128)}, f32[6,34,18,1]{3,2,1,0:T(8,128)}) fusion(f32[6,34,18,128]{3,2,1,0:T(8,128)S(1)} %pad_maximum_fusion), kind=kLoop, calls=%fused_computation.227 | loop fusion | bytes 58752 | tf_op jit(solution)/shard_map/slice | solution.py:12
  22.8 2.6 %copy.58 = f32[6,34,18,1]{1,3,2,0:T(1,128)S(1)} copy(f32[6,34,18,1]{3,2,1,0:T(8,128)} %get-tuple-element.152) | data formatting | bytes 29376 | tf_op jit(solution)/shard_map/slice | solution.py:12
  26.8 2.6 %copy.59 = f32[6,34,18,1]{1,3,2,0:T(1,128)S(1)} copy(f32[6,34,18,1]{3,2,1,0:T(8,128)} %get-tuple-element.153) | data formatting | bytes 29376 | tf_op jit(solution)/shard_map/slice | solution.py:11
  29.4 4.5 %collective-permute-start.5 = (f32[6,34,18,1]{1,3,2,0:T(1,128)S(1)}, f32[6,34,18,1]{1,3,2,0:T(1,128)S(1)}, u32[]{:S(2)}, u32[]{:S(2)}) collective-permute-start(f32[6,34,18,1]{1,3,2,0:T(1,128)S(1)} %copy.59), channel_id=1, source_target_pairs={{1,0},{2,1},{3,2},{5,4},{6,5},{7,6},{9,8},{10,9},{11,10},{13,12},{... | collective-permute-start | bytes 44072 | tf_op jit(solution)/shard_map/ppermute | solution.py:17
  33.9 2.6 %copy.60 = f32[6,34,18,1]{3,2,1,0:T(8,128)} copy(f32[6,34,18,1]{1,3,2,0:T(1,128)S(1)} %collective-permute-done.4) | data formatting | bytes 29376 | tf_op jit(solution)/shard_map/ppermute | solution.py:15
  36.5 2.6 %copy.61 = f32[6,34,18,1]{3,2,1,0:T(8,128)} copy(f32[6,34,18,1]{1,3,2,0:T(1,128)S(1)} %collective-permute-done.5) | data formatting | bytes 29376 | tf_op jit(solution)/shard_map/ppermute | solution.py:17
  43.1 4.9 %fusion.37 = f32[5,32,16,128]{3,2,1,0:T(8,128)S(1)} fusion(f32[5,32,16,128]{3,2,1,0:T(8,128)S(1)} %copy-done, f32[6,34,18,1]{3,2,1,0:T(8,128)S(1)} %copy-done.2, f32[6,34,1,128]{3,2,1,0:T(1,128)S(1)} %copy-done.15, f32[6,34,1,128]{3,2,1,0:T(1,128)S(1)} %collective-permute-done.2, f32[6,1,16,128]{3,2,1,0:T(8,128)S(1)} %copy-done.19, ...), kind=kLoop, calls=%fused_computation.74 | loop fusion | flops 16711680 | bytes 4793084 | tf_op jit(solution)/shard_map/sub | solution.py:42
  49.3 4.5 %collective-permute-start.7 = (f32[5,1,16,128]{3,2,1,0:T(8,128)S(1)}, f32[5,1,16,128]{3,2,1,0:T(8,128)S(1)}, u32[]{:S(2)}, u32[]{:S(2)}) collective-permute-start(f32[5,1,16,128]{3,2,1,0:T(8,128)S(1)} %get-tuple-element.166), channel_id=1, source_target_pairs={{0,32},{32,64},{64,96},{96,128},{128,160},{160,192},{192,224},{1,3... | collective-permute-start | bytes 122888 | tf_op jit(solution)/shard_map/ppermute | solution.py:15
  60.2 3.5 %collective-permute-done.9 = f32[5,34,1,128]{3,2,1,0:T(1,128)S(1)} collective-permute-done((f32[5,34,1,128]{3,2,1,0:T(1,128)S(1)}, f32[5,34,1,128]{3,2,1,0:T(1,128)S(1)}, u32[]{:S(2)}, u32[]{:S(2)}) %collective-permute-start.9) | collective-permute-done | bytes 87072 | tf_op jit(solution)/shard_map/ppermute | solution.py:15
  64.0 2.6 %fusion.101 = (f32[5,34,18,1]{3,2,1,0:T(8,128)}, f32[5,34,18,1]{3,2,1,0:T(8,128)}) fusion(f32[5,34,18,128]{3,2,1,0:T(8,128)S(1)} %pad_maximum_fusion.1), kind=kLoop, calls=%fused_computation.228 | loop fusion | bytes 48960 | tf_op jit(solution)/shard_map/slice | solution.py:12
  69.0 3.2 %collective-permute-start.10 = (f32[5,34,18,1]{1,3,2,0:T(1,128)S(1)}, f32[5,34,18,1]{1,3,2,0:T(1,128)S(1)}, u32[]{:S(2)}, u32[]{:S(2)}) collective-permute-start(f32[5,34,18,1]{1,3,2,0:T(1,128)S(1)} %copy.64), channel_id=1, source_target_pairs={{1,0},{2,1},{3,2},{5,4},{6,5},{7,6},{9,8},{10,9},{11,10},{13,12},{... | collective-permute-start | bytes 36728 | tf_op jit(solution)/shard_map/ppermute | solution.py:17
  78.1 2.3 collective-permute-done.11
  82.8 5.3 %fusion.14 = f32[5,32,16,128]{3,2,1,0:T(8,128)S(1)} fusion(f32[5,32,16,128]{3,2,1,0:T(8,128)S(1)} %fusion.37, f32[5,34,18,1]{3,2,1,0:T(8,128)} %copy.65, f32[5,34,1,128]{3,2,1,0:T(1,128)S(1)} %collective-permute-done.8, f32[5,34,1,128]{3,2,1,0:T(1,128)S(1)} %collective-permute-done.9, f32[5,1,16,128]{3,2,1,0:T(8,128)S(1)} %collective-permute-done.6, ...), kind=kLoop, calls=%fused_computation.32 | loop fusion | flops 14745600 | bytes 4474844 | tf_op jit(solution)/shard_map/sub | solution.py:42
  89.8 5.5 %collective-permute-start.13 = (f32[1,16,128]{2,1,0:T(8,128)S(1)}, f32[1,16,128]{2,1,0:T(8,128)S(1)}, u32[]{:S(2)}, u32[]{:S(2)}) collective-permute-start(f32[1,16,128]{2,1,0:T(8,128)S(1)} %get-tuple-element.162), channel_id=1, source_target_pairs={{0,32},{32,64},{64,96},{96,128},{128,160},{160,192},{192,224},{1,3... | collective-permute-start | bytes 24584 | tf_op jit(solution)/shard_map/ppermute | solution.py:15
  98.6 2.4 collective-permute-start.15
  101.0 2.6 %collective-permute-done.15 = f32[34,1,128]{2,1,0:T(1,128)S(1)} collective-permute-done((f32[34,1,128]{2,1,0:T(1,128)S(1)}, f32[34,1,128]{2,1,0:T(1,128)S(1)}, u32[]{:S(2)}, u32[]{:S(2)}) %collective-permute-start.15) | collective-permute-done | bytes 17440 | tf_op jit(solution)/shard_map/ppermute | solution.py:15
  104.8 3.5 %collective-permute-start.16 = (f32[34,18,1]{2,1,0:T(8,128)}, f32[34,18,1]{2,1,0:T(8,128)}, u32[]{:S(2)}, u32[]{:S(2)}) collective-permute-start(f32[34,18,1]{2,1,0:T(8,128)} %get-tuple-element.182), channel_id=1, source_target_pairs={{1,0},{2,1},{3,2},{5,4},{6,5},{7,6},{9,8},{10,9},{11,10},{13,12},{... | collective-permute-start | bytes 7352 | tf_op jit(solution)/shard_map/ppermute | solution.py:17
  110.0 6.6 %collective-permute-done.16 = f32[34,18,1]{2,1,0:T(8,128)} collective-permute-done((f32[34,18,1]{2,1,0:T(8,128)}, f32[34,18,1]{2,1,0:T(8,128)}, u32[]{:S(2)}, u32[]{:S(2)}) %collective-permute-start.16) | collective-permute-done | bytes 2480 | tf_op jit(solution)/shard_map/ppermute | solution.py:17
  116.5 4.9 %collective-permute-done.17 = f32[34,18,1]{2,1,0:T(8,128)} collective-permute-done((f32[34,18,1]{2,1,0:T(8,128)}, f32[34,18,1]{2,1,0:T(8,128)}, u32[]{:S(2)}, u32[]{:S(2)}) %collective-permute-start.17) | collective-permute-done | bytes 2480 | tf_op jit(solution)/shard_map/ppermute | solution.py:15
  123.2 92.2 %while.11 = (s32[]{:T(128)}, f32[16,16,4,128]{3,1,0,2:T(8,128)S(1)}, f32[16]{0:T(128)S(1)}, f32[16]{0:T(128)S(1)}, f32[16]{0:T(128)S(1)}, /*index=5*/f32[32,16,1...) while((s32[]{:T(128)}, ...), condition=%wide.region_3.4_spmd.clone, body=%wide.region_0.3_spmd.clone.sunk | while | flops 26882052 | bytes 3047637 | solution.py:96
  216.8 29.0 %all_to_all.5 = f32[8,32,4,128]{3,2,1,0:T(4,128)S(1)} all-to-all(f32[8,32,4,128]{3,2,1,0:T(4,128)S(1)} %bitcast.92), channel_id=1, replica_groups=mesh['gz'=8,'gy'=8,'gx'=4] {'gz'}, dimensions={0} | all-to-all | bytes 1048576 | tf_op jit(solution)/shard_map/all_to_all | solution.py:103
  (292 shorter events, 125.1 us)
Async XLA Ops:
  1.6 5.6 %collective-permute-start = (f32[6,1,16,128]{3,2,1,0:T(8,128)S(1)}, f32[6,1,16,128]{3,2,1,0:T(8,128)S(1)}, u32[]{:S(2)}, u32[]{:S(2)}) collective-permute-start(f32[6,1,16,128]{3,2,1,0:T(8,128)S(1)} %get-tuple-element.158), channel_id=1, source_target_pairs={{0,32},{32,64},{64,96},{96,128},{128,160},{160,192},{192,224},{1,3... | collective-permute-start | bytes 147464 | tf_op jit(solution)/shard_map/ppermute | solution.py:15
  5.4 6.0 %collective-permute-start.1 = (f32[6,1,16,128]{3,2,1,0:T(8,128)S(1)}, f32[6,1,16,128]{3,2,1,0:T(8,128)S(1)}, u32[]{:S(2)}, u32[]{:S(2)}) collective-permute-start(f32[6,1,16,128]{3,2,1,0:T(8,128)S(1)} %get-tuple-element.159), channel_id=1, source_target_pairs={{32,0},{64,32},{96,64},{128,96},{160,128},{192,160},{224,192},{33,... | collective-permute-start | bytes 147464 | tf_op jit(solution)/shard_map/ppermute | solution.py:17
  7.2 32.0 %copy-start.16 = (f32[6,1,16,128]{3,2,1,0:T(8,128)}, f32[6,1,16,128]{3,2,1,0:T(8,128)S(1)}, u32[]{:S(2)}) copy-start(f32[6,1,16,128]{3,2,1,0:T(8,128)S(1)} %collective-permute-done) | copy-start | bytes 147460
  11.4 27.7 %copy-start.18 = (f32[6,1,16,128]{3,2,1,0:T(8,128)}, f32[6,1,16,128]{3,2,1,0:T(8,128)S(1)}, u32[]{:S(2)}) copy-start(f32[6,1,16,128]{3,2,1,0:T(8,128)S(1)} %collective-permute-done.1) | copy-start | bytes 147460
  11.6 6.0 %collective-permute-start.2 = (f32[6,34,1,128]{3,2,1,0:T(1,128)S(1)}, f32[6,34,1,128]{3,2,1,0:T(1,128)S(1)}, u32[]{:S(2)}, u32[]{:S(2)}) collective-permute-start(f32[6,34,1,128]{3,2,1,0:T(1,128)S(1)} %get-tuple-element.156), channel_id=1, source_target_pairs={{0,4},{4,8},{8,12},{12,16},{16,20},{20,24},{24,28},{1,5},{5,9},{9,... | collective-permute-start | bytes 313352 | tf_op jit(solution)/shard_map/ppermute | solution.py:15
  13.5 5.9 %collective-permute-start.3 = (f32[6,34,1,128]{3,2,1,0:T(1,128)S(1)}, f32[6,34,1,128]{3,2,1,0:T(1,128)S(1)}, u32[]{:S(2)}, u32[]{:S(2)}) collective-permute-start(f32[6,34,1,128]{3,2,1,0:T(1,128)S(1)} %get-tuple-element.157), channel_id=1, source_target_pairs={{4,0},{8,4},{12,8},{16,12},{20,16},{24,20},{28,24},{5,1},{9,5},{13... | collective-permute-start | bytes 313352 | tf_op jit(solution)/shard_map/ppermute | solution.py:17
  19.4 19.7 %copy-start.14 = (f32[6,34,1,128]{3,2,1,0:T(1,128)}, f32[6,34,1,128]{3,2,1,0:T(1,128)S(1)}, u32[]{:S(2)}) copy-start(f32[6,34,1,128]{3,2,1,0:T(1,128)S(1)} %collective-permute-done.3) | copy-start | bytes 313348
  25.4 8.6 %collective-permute-start.4 = (f32[6,34,18,1]{1,3,2,0:T(1,128)S(1)}, f32[6,34,18,1]{1,3,2,0:T(1,128)S(1)}, u32[]{:S(2)}, u32[]{:S(2)}) collective-permute-start(f32[6,34,18,1]{1,3,2,0:T(1,128)S(1)} %copy.58), channel_id=1, source_target_pairs={{0,1},{1,2},{2,3},{4,5},{5,6},{6,7},{8,9},{9,10},{10,11},{12,13},{... | collective-permute-start | bytes 44072 | tf_op jit(solution)/shard_map/ppermute | solution.py:15
  29.4 7.2 %collective-permute-start.5 = (f32[6,34,18,1]{1,3,2,0:T(1,128)S(1)}, f32[6,34,18,1]{1,3,2,0:T(1,128)S(1)}, u32[]{:S(2)}, u32[]{:S(2)}) collective-permute-start(f32[6,34,18,1]{1,3,2,0:T(1,128)S(1)} %copy.59), channel_id=1, source_target_pairs={{1,0},{2,1},{3,2},{5,4},{6,5},{7,6},{9,8},{10,9},{11,10},{13,12},{... | collective-permute-start | bytes 44072 | tf_op jit(solution)/shard_map/ppermute | solution.py:17
  48.0 6.0 %collective-permute-start.6 = (f32[5,1,16,128]{3,2,1,0:T(8,128)S(1)}, f32[5,1,16,128]{3,2,1,0:T(8,128)S(1)}, u32[]{:S(2)}, u32[]{:S(2)}) collective-permute-start(f32[5,1,16,128]{3,2,1,0:T(8,128)S(1)} %get-tuple-element.167), channel_id=1, source_target_pairs={{32,0},{64,32},{96,64},{128,96},{160,128},{192,160},{224,192},{33,... | collective-permute-start | bytes 122888 | tf_op jit(solution)/shard_map/ppermute | solution.py:17
  49.3 6.4 %collective-permute-start.7 = (f32[5,1,16,128]{3,2,1,0:T(8,128)S(1)}, f32[5,1,16,128]{3,2,1,0:T(8,128)S(1)}, u32[]{:S(2)}, u32[]{:S(2)}) collective-permute-start(f32[5,1,16,128]{3,2,1,0:T(8,128)S(1)} %get-tuple-element.166), channel_id=1, source_target_pairs={{0,32},{32,64},{64,96},{96,128},{128,160},{160,192},{192,224},{1,3... | collective-permute-start | bytes 122888 | tf_op jit(solution)/shard_map/ppermute | solution.py:15
  55.9 4.3 %collective-permute-start.8 = (f32[5,34,1,128]{3,2,1,0:T(1,128)S(1)}, f32[5,34,1,128]{3,2,1,0:T(1,128)S(1)}, u32[]{:S(2)}, u32[]{:S(2)}) collective-permute-start(f32[5,34,1,128]{3,2,1,0:T(1,128)S(1)} %get-tuple-element.161), channel_id=1, source_target_pairs={{4,0},{8,4},{12,8},{16,12},{20,16},{24,20},{28,24},{5,1},{9,5},{13... | collective-permute-start | bytes 261128 | tf_op jit(solution)/shard_map/ppermute | solution.py:17
  57.9 5.8 %collective-permute-start.9 = (f32[5,34,1,128]{3,2,1,0:T(1,128)S(1)}, f32[5,34,1,128]{3,2,1,0:T(1,128)S(1)}, u32[]{:S(2)}, u32[]{:S(2)}) collective-permute-start(f32[5,34,1,128]{3,2,1,0:T(1,128)S(1)} %get-tuple-element.160), channel_id=1, source_target_pairs={{0,4},{4,8},{8,12},{12,16},{16,20},{20,24},{24,28},{1,5},{5,9},{9,... | collective-permute-start | bytes 261128 | tf_op jit(solution)/shard_map/ppermute | solution.py:15
  69.0 6.9 %collective-permute-start.10 = (f32[5,34,18,1]{1,3,2,0:T(1,128)S(1)}, f32[5,34,18,1]{1,3,2,0:T(1,128)S(1)}, u32[]{:S(2)}, u32[]{:S(2)}) collective-permute-start(f32[5,34,18,1]{1,3,2,0:T(1,128)S(1)} %copy.64), channel_id=1, source_target_pairs={{1,0},{2,1},{3,2},{5,4},{6,5},{7,6},{9,8},{10,9},{11,10},{13,12},{... | collective-permute-start | bytes 36728 | tf_op jit(solution)/shard_map/ppermute | solution.py:17
  74.5 5.9 %collective-permute-start.11 = (f32[5,34,18,1]{1,3,2,0:T(1,128)S(1)}, f32[5,34,18,1]{1,3,2,0:T(1,128)S(1)}, u32[]{:S(2)}, u32[]{:S(2)}) collective-permute-start(f32[5,34,18,1]{1,3,2,0:T(1,128)S(1)} %copy.66), channel_id=1, source_target_pairs={{0,1},{1,2},{2,3},{4,5},{5,6},{6,7},{8,9},{9,10},{10,11},{12,13},{... | collective-permute-start | bytes 36728 | tf_op jit(solution)/shard_map/ppermute | solution.py:15
  88.1 16.6 %copy-start.4 = (f32[5,32,16,128]{3,2,1,0:T(8,128)}, f32[5,32,16,128]{3,2,1,0:T(8,128)S(1)}, u32[]{:S(2)}) copy-start(f32[5,32,16,128]{3,2,1,0:T(8,128)S(1)} %fusion.14) | copy-start | bytes 3932164
  88.2 7.1 %collective-permute-start.12 = (f32[1,16,128]{2,1,0:T(8,128)S(1)}, f32[1,16,128]{2,1,0:T(8,128)S(1)}, u32[]{:S(2)}, u32[]{:S(2)}) collective-permute-start(f32[1,16,128]{2,1,0:T(8,128)S(1)} %get-tuple-element.163), channel_id=1, source_target_pairs={{32,0},{64,32},{96,64},{128,96},{160,128},{192,160},{224,192},{33,... | collective-permute-start | bytes 24584 | tf_op jit(solution)/shard_map/ppermute | solution.py:17
  89.8 6.8 %collective-permute-start.13 = (f32[1,16,128]{2,1,0:T(8,128)S(1)}, f32[1,16,128]{2,1,0:T(8,128)S(1)}, u32[]{:S(2)}, u32[]{:S(2)}) collective-permute-start(f32[1,16,128]{2,1,0:T(8,128)S(1)} %get-tuple-element.162), channel_id=1, source_target_pairs={{0,32},{32,64},{64,96},{96,128},{128,160},{160,192},{192,224},{1,3... | collective-permute-start | bytes 24584 | tf_op jit(solution)/shard_map/ppermute | solution.py:15
  96.6 4.4 %collective-permute-start.14 = (f32[34,1,128]{2,1,0:T(1,128)S(1)}, f32[34,1,128]{2,1,0:T(1,128)S(1)}, u32[]{:S(2)}, u32[]{:S(2)}) collective-permute-start(f32[34,1,128]{2,1,0:T(1,128)S(1)} %get-tuple-element.185), channel_id=1, source_target_pairs={{4,0},{8,4},{12,8},{16,12},{20,16},{24,20},{28,24},{5,1},{9,5},{13... | collective-permute-start | bytes 52232 | tf_op jit(solution)/shard_map/ppermute | solution.py:17
  98.6 5.1 %collective-permute-start.15 = (f32[34,1,128]{2,1,0:T(1,128)S(1)}, f32[34,1,128]{2,1,0:T(1,128)S(1)}, u32[]{:S(2)}, u32[]{:S(2)}) collective-permute-start(f32[34,1,128]{2,1,0:T(1,128)S(1)} %get-tuple-element.184), channel_id=1, source_target_pairs={{0,4},{4,8},{8,12},{12,16},{16,20},{20,24},{24,28},{1,5},{5,9},{9,... | collective-permute-start | bytes 52232 | tf_op jit(solution)/shard_map/ppermute | solution.py:15
  104.8 18.2 %copy-start.5 = (f32[5,32,16,128]{3,2,1,0:T(8,128)S(1)}, f32[5,32,16,128]{3,2,1,0:T(8,128)}, u32[]{:S(2)}) copy-start(f32[5,32,16,128]{3,2,1,0:T(8,128)} %copy-done.4) | copy-start | bytes 3932164
  104.8 11.7 %collective-permute-start.16 = (f32[34,18,1]{2,1,0:T(8,128)}, f32[34,18,1]{2,1,0:T(8,128)}, u32[]{:S(2)}, u32[]{:S(2)}) collective-permute-start(f32[34,18,1]{2,1,0:T(8,128)} %get-tuple-element.182), channel_id=1, source_target_pairs={{1,0},{2,1},{3,2},{5,4},{6,5},{7,6},{9,8},{10,9},{11,10},{13,12},{... | collective-permute-start | bytes 7352 | tf_op jit(solution)/shard_map/ppermute | solution.py:17
  108.3 13.1 %collective-permute-start.17 = (f32[34,18,1]{2,1,0:T(8,128)}, f32[34,18,1]{2,1,0:T(8,128)}, u32[]{:S(2)}, u32[]{:S(2)}) collective-permute-start(f32[34,18,1]{2,1,0:T(8,128)} %get-tuple-element.183), channel_id=1, source_target_pairs={{0,1},{1,2},{2,3},{4,5},{5,6},{6,7},{8,9},{9,10},{10,11},{12,13},{... | collective-permute-start | bytes 7352 | tf_op jit(solution)/shard_map/ppermute | solution.py:15
  109.9 13.2 %copy-start.24 = (f32[16]{0:T(128)S(1)}, f32[16]{0:T(128)}, u32[]{:S(2)}) copy-start(f32[16]{0:T(128)} %param.16) | copy-start | bytes 196
  (21 other events, 151.0 us)
where the time goes:
time: 249 us; the launch traced here: 247 us
  local copies, waits for them, and re-layouts  60.9 us (24%)
  starting transfers between devices  47.5 us (19%)
  other arithmetic  41 us (16%)
  waiting for transfers between devices  30 us (12%)
  blocking collectives  29 us (12%)
  matrix products  27.2 us (11%)
  loops' own time  10.1 us (4%)
    all_to_all x1, blocking collectives, shards(): lax.all_to_all(grouped, 'gz', split_axis=0, concat_axis=0, tiled=True)  29 us
    dynamic_slice x48, local copies, waits for them, and re-layouts, shards(): rendered = lax.map(render, (tf_center, tf_sharp, tf_gain, tf_color.T))  28.7 us
    dot_general x16, matrix products, render(): jnp.einsum('wz,zyx->wyx', earlier, depth, precision=lax.Precision.HIGHEST)  27.2 us
    ppermute x9, starting transfers between devices, extended(): lax.ppermute(tail, axis, [(i, (i + 1) % count) for i in range(ends)])  24.4 us
    ppermute x9, starting transfers between devices, extended(): lax.ppermute(head, axis, [((i + 1) % count, i) for i in range(ends)])  23.1 us
    reduce_sum x16, other arithmetic, render(): alpha = 1.0 - jnp.exp(-jnp.sum(depth, axis=0))  21 us
    ppermute x9, waiting for transfers between devices, extended(): lax.ppermute(tail, axis, [(i, (i + 1) % count) for i in range(ends)])  17.2 us
    ppermute x9, waiting for transfers between devices, extended(): lax.ppermute(head, axis, [((i + 1) % count, i) for i in range(ends)])  12.8 us
  transfers between devices with their start and end apart: 18, of which 12 were waited for; matrix products, arithmetic and copies ran while one was open for 4% of the time, Pallas kernels for 0%

commit v1 on v0

v1 whole, which is shorter than its diff:
```python
import functools
import math

import jax
import jax.numpy as jnp
from jax import lax
from jax.experimental import pallas as pl
from jax.experimental.pallas import tpu as pltpu
from jax.sharding import PartitionSpec as P

MESH = pl.DeviceIdType.MESH
LOG2E = math.log2(math.e)
NF, CZ, CY, CX, TF = 5, 32, 16, 128, 16
R0 = 8
TILES = TF * CY


def kernel(
    fields, kappa, courant, center, sharp, gain, color, mask, perm,
    adv_out, pic_out,
    u0, u1, u2, sp, ysend1, yhalo1, xsend1, xhalo1, ysend2, yhalo2, xsend2, xhalo2,
    ysend3, yhalo3, xsend3, xhalo3, rs, rm, rb, tiles, recv,
    send_sem, recv_sem, tile_send, tile_recv, local_sem,
):
    f32 = jnp.float32
    nz = lax.axis_size("gz")
    sizes = [lax.axis_size(a) for a in ("gz", "gy", "gx")]
    mes = [lax.axis_index(a) for a in ("gz", "gy", "gx")]
    names = ("gz", "gy", "gx")
    per_owner = TILES // nz

    load_f = pltpu.make_async_copy(fields, u0.at[pl.ds(0, NF), pl.ds(1, CZ), pl.ds(R0, CY), :], local_sem.at[0])
    load_k = pltpu.make_async_copy(kappa, u0.at[NF, pl.ds(1, CZ), pl.ds(R0, CY), :], local_sem.at[1])
    load_f.start()
    load_k.start()

    barrier = pltpu.get_barrier_semaphore()
    count = jnp.int32(nz - 1)
    for off in range(1, nz):
        pl.semaphore_signal(
            barrier, inc=1, device_id={"gz": lax.rem(mes[0] + off, nz)}, device_id_type=MESH
        )
    for a in (1, 2):
        for step in (-1, 1):
            ok = (mes[a] > 0) if step < 0 else (mes[a] < sizes[a] - 1)

            @pl.when(ok)
            def _(a=a, step=step):
                pl.semaphore_signal(
                    barrier, inc=1, device_id={names[a]: mes[a] + step}, device_id_type=MESH
                )

            count = count + ok.astype(jnp.int32)
    pl.semaphore_wait(barrier, count)

    def exists(a, side):
        return (mes[a] > 0) if side == 0 else (mes[a] < sizes[a] - 1)

    class Face:
        def __init__(self, a, side, sem, src, dst):
            self.a, self.side, self.sem, self.src, self.dst = a, side, sem, src, dst

        def desc(self):
            a, side = self.a, self.side
            return pltpu.make_async_remote_copy(
                src_ref=self.src, dst_ref=self.dst,
                send_sem=send_sem.at[self.sem], recv_sem=recv_sem.at[self.sem],
                device_id={names[a]: mes[a] + (-1 if side == 0 else 1)}, device_id_type=MESH,
            )

        def start(self):
            @pl.when(exists(self.a, self.side))
            def _():
                self.desc().start()

        def wait_recv(self, zero):
            got = exists(self.a, 1 - self.side)

            @pl.when(got)
            def _():
                self.desc().wait_recv()

            @pl.when(jnp.logical_not(got))
            def _():
                zero()

        def wait_send(self):
            @pl.when(exists(self.a, self.side))
            def _():
                self.desc().wait_send()

    def zero_of(ref):
        def zero():
            ref[...] = jnp.zeros(ref.shape, f32)
        return zero

    lane = lax.broadcasted_iota(jnp.int32, (8, 128), 1)
    sub = lax.broadcasted_iota(jnp.int32, (8, 128), 0)
    pair = lax.bitwise_and(lax.shift_right_logical(lane + 1, 1), 63)
    even = lax.bitwise_and(lane, 1) == 0
    first_lane, last_lane = lane == 0, lane == CX - 1
    first_row, last_row = sub == 0, sub == 7

    def rolled(x, shift):
        return pltpu.roll(x, shift, 1)

    def packed(value, into, v):
        return jnp.where(pair == v, rolled(value, 2 * v), into)

    def halo_pack(ref, f):
        return jnp.where(even, rolled(ref[0, f], 1), rolled(ref[1, f], CX - 1))

    waits = []

    def faces(buf, sem, ysend, yhalo, xsend, xhalo, z_list):
        out = []
        for i, (side, src, dst) in enumerate(z_list):
            out.append((Face(0, side, sem + i, src, dst), dst))
        base = sem + len(z_list)
        for side in (0, 1):
            out.append((Face(1, side, base + side, ysend.at[side], yhalo.at[1 - side]), yhalo.at[1 - side]))
            out.append((Face(2, side, base + 2 + side, xsend.at[side], xhalo.at[1 - side]), xhalo.at[1 - side]))
        return out

    rows = pl.ds(R0, CY)
    r1 = faces(
        u0, 0, ysend1, yhalo1, xsend1, xhalo1,
        [
            (0, fields.at[:, 0], u0.at[pl.ds(0, NF), CZ + 1, rows, :]),
            (1, fields.at[:, CZ - 1], u0.at[pl.ds(0, NF), 0, rows, :]),
            (0, kappa.at[0], u0.at[NF, CZ + 1, rows, :]),
            (1, kappa.at[CZ - 1], u0.at[NF, 0, rows, :]),
        ],
    )
    for face, _ in r1[:4]:
        face.start()
    load_f.wait()
    load_k.wait()

    def pack1(z, q):
        q = list(q)
        for f in range(NF + 1):
            ysend1[0, f, pl.ds(z, 1), :] = u0[f, z + 1, pl.ds(R0, 1), :]
            ysend1[1, f, pl.ds(z, 1), :] = u0[f, z + 1, pl.ds(R0 + CY - 1, 1), :]
            for h in range(2):
                q[f] = packed(u0[f, z + 1, pl.ds(R0 + 8 * h, 8), :], q[f], 2 * z + h)
        return tuple(q)

    q = lax.fori_loop(0, CZ, pack1, tuple(jnp.zeros((8, 128), f32) for _ in range(NF + 1)))
    for f in range(NF + 1):
        xsend1[0, f] = q[f]
        xsend1[1, f] = q[f]
    for face, _ in r1[4:]:
        face.start()
    for face, dst in r1:
        face.wait_recv(zero_of(dst))
    waits += r1

    def advance(src, yhalo, xhalo, emit):
        kp = 0.5 * halo_pack(xhalo1, NF)
        fp = [halo_pack(xhalo, f) for f in range(NF)]
        cz = [courant[f, 0] for f in range(NF)]
        cy = [courant[f, 1] for f in range(NF)]
        cx = [courant[f, 2] for f in range(NF)]
        rest = [1.0 - (cz[f] + cy[f] + cx[f]) for f in range(NF)]

        def around(ref, f, z, h, yh, pack, shift, scale):
            row = R0 + 8 * h
            mid = ref[f, z + 1, pl.ds(row, 8), :]
            zm = ref[f, z, pl.ds(row, 8), :]
            zp = ref[f, z + 2, pl.ds(row, 8), :]
            ym = ref[f, z + 1, pl.ds(row - 1, 8), :]
            yp = ref[f, z + 1, pl.ds(row + 1, 8), :]
            if h == 0:
                ym = jnp.where(first_row, jnp.broadcast_to(yh[0, f, pl.ds(z, 1), :], (8, 128)), ym)
            else:
                yp = jnp.where(last_row, jnp.broadcast_to(yh[1, f, pl.ds(z, 1), :], (8, 128)), yp)
            if scale:
                mid, zm, zp, ym, yp = [0.5 * w for w in (mid, zm, zp, ym, yp)]
            edge = rolled(pack, shift)
            xm = jnp.where(first_lane, edge, rolled(mid, 1))
            xp = jnp.where(last_lane, edge, rolled(mid, CX - 1))
            return mid, zm, zp, ym, yp, xm, xp

        def body(z, q):
            q = list(q)
            for h in range(2):
                v = 2 * z + h
                shift = lax.rem(128 - 2 * v, 128)
                k = around(u0, NF, z, h, yhalo1, kp, shift, True)
                kzm, kzp, kym, kyp, kxm, kxp = [k[0] + w for w in k[1:]]
                ksum = (kzm + kzp) + (kym + kyp) + (kxm + kxp)
                for f in range(NF):
                    mid, zm, zp, ym, yp, xm, xp = around(src, f, z, h, yhalo, fp[f], shift, False)
                    value = (
                        (rest[f] - ksum) * mid
                        + (kzp * zp + (kzm + cz[f]) * zm)
                        + (kyp * yp + (kym + cy[f]) * ym)
                        + (kxp * xp + (kxm + cx[f]) * xm)
                    )
                    emit(f, z, h, value)
                    q[f] = packed(value, q[f], v)
            return tuple(q)

        return lax.fori_loop(0, CZ, body, tuple(jnp.zeros((8, 128), f32) for _ in range(NF)))

    def emit1(f, z, h, value):
        u1[f, z + 1, pl.ds(R0 + 8 * h, 8), :] = value
        side, row = (0, 0) if h == 0 else (1, 7)
        ysend2[side, f, pl.ds(z, 1), :] = value[row : row + 1, :]

    q = advance(u0, yhalo1, xhalo1, emit1)
    for f in range(NF):
        xsend2[0, f] = q[f]
        xsend2[1, f] = q[f]
    r2 = faces(
        u1, 8, ysend2, yhalo2, xsend2, xhalo2,
        [
            (0, u1.at[:, 1, rows, :], u1.at[:, CZ + 1, rows, :]),
            (1, u1.at[:, CZ, rows, :], u1.at[:, 0, rows, :]),
        ],
    )
    for face, _ in r2:
        face.start()
    for face, dst in r2:
        face.wait_recv(zero_of(dst))
    waits += r2

    def emit2(f, z, h, value):
        u2[f, z, pl.ds(8 * h, 8), :] = value
        if f == 0:
            sp[z + 1, pl.ds(R0 + 8 * h, 8), :] = value
            side, row = (0, 0) if h == 0 else (1, 7)
            ysend3[side, 0, pl.ds(z, 1), :] = value[row : row + 1, :]

    q = advance(u1, yhalo2, xhalo2, emit2)
    xsend3[0, 0] = q[0]
    xsend3[1, 0] = q[0]
    r3 = faces(
        sp, 14, ysend3, yhalo3, xsend3, xhalo3,
        [
            (0, sp.at[1, rows, :], sp.at[CZ + 1, rows, :]),
            (1, sp.at[CZ, rows, :], sp.at[0, rows, :]),
        ],
    )
    for face, _ in r3:
        face.start()
    store = pltpu.make_async_copy(u2, adv_out, local_sem.at[2])
    store.start()

    def sites(z, h):
        start = h * 8 * CZ + lax.rem(z, 4) * 8 + lax.div(z, 4)
        return pl.ds(start, 8, stride=CZ)

    rs2, rm2 = rs.reshape(CY * CZ, CX), rm.reshape(CY * CZ, CX)
    rb2 = rb.reshape(3, CY * CZ, CX)

    def modulate(z, carry):
        for h in range(2):
            at = sites(z, h)
            rs2[at, :] = u2[0, z, pl.ds(8 * h, 8), :]
            rm2[at, :] = (-LOG2E) * (1.0 + 0.5 * jnp.tanh(u2[4, z, pl.ds(8 * h, 8), :]))
        return carry

    lax.fori_loop(0, CZ, modulate, 0)
    for face, dst in r3:
        face.wait_recv(zero_of(dst))
    waits += r3

    spack = halo_pack(xhalo3, 0)

    def shading(z, carry):
        for h in range(2):
            row = R0 + 8 * h
            v = 2 * z + h
            mid = sp[z + 1, pl.ds(row, 8), :]
            ym = sp[z + 1, pl.ds(row - 1, 8), :]
            yp = sp[z + 1, pl.ds(row + 1, 8), :]
            if h == 0:
                ym = jnp.where(first_row, jnp.broadcast_to(yhalo3[0, 0, pl.ds(z, 1), :], (8, 128)), ym)
            else:
                yp = jnp.where(last_row, jnp.broadcast_to(yhalo3[1, 0, pl.ds(z, 1), :], (8, 128)), yp)
            edge = rolled(spack, lax.rem(128 - 2 * v, 128))
            xm = jnp.where(first_lane, edge, rolled(mid, 1))
            xp = jnp.where(last_lane, edge, rolled(mid, CX - 1))
            gz = 0.5 * (sp[z + 2, pl.ds(row, 8), :] - sp[z, pl.ds(row, 8), :])
            gy = 0.5 * (yp - ym)
            gx = 0.5 * (xp - xm)
            shade = 0.35 + 0.65 * jnp.abs(0.64 * gz + 0.6 * gy + 0.48 * gx) * lax.rsqrt(
                gz * gz + gy * gy + gx * gx + 1.0
            )
            at = sites(z, h)
            for k in range(3):
                rb2[k, at, :] = shade * jax.nn.sigmoid(u2[1 + k, z, pl.ds(8 * h, 8), :])
        return carry

    lax.fori_loop(0, CZ, shading, 0)

    def owner_copy(k, owner):
        return pltpu.make_async_remote_copy(
            src_ref=tiles.at[k], dst_ref=recv.at[mes[0]],
            send_sem=tile_send.at[k], recv_sem=tile_recv.at[mes[0]],
            device_id={"gz": owner}, device_id_type=MESH,
        )

    def render(owner, dst):
        def one(i, carry):
            p = perm[0, 0, owner * per_owner + i]
            t = lax.shift_right_logical(p, 4)
            y = lax.bitwise_and(p, 15)
            cover = mask[0, t, y, 0].astype(f32)
            mid, slope, amount = center[t], -LOG2E * sharp[t], gain[t]
            gap = rs[y] - mid
            depth = jnp.exp2(slope * (gap * gap)) * (amount * rm[y])
            e = [depth[0:8]]
            for w in range(1, 4):
                e.append(e[-1] + depth[8 * w : 8 * w + 8])
            inclusive = e[3]
            for sh in (1, 2, 4):
                inclusive = inclusive + jnp.where(sub >= sh, pltpu.roll(inclusive, sh, 0), 0.0)
            before = jnp.exp2(inclusive - e[3])
            lit = [jnp.exp2(x) for x in e]
            weight = [1.0 - lit[0]] + [lit[w] - lit[w + 1] for w in range(3)]
            for k in range(3):
                base = rb[k, y]
                total = weight[0] * base[0:8]
                for w in range(1, 4):
                    total = total + weight[w] * base[8 * w : 8 * w + 8]
                total = jnp.sum(total * before, axis=0, keepdims=True)
                dst[k, pl.ds(i, 1), :] = total * (color[k, t] * cover)
            dst[3, pl.ds(i, 1), :] = (1.0 - jnp.exp2(inclusive[7:8])) * cover
            return carry

        lax.fori_loop(0, per_owner, one, 0, unroll=2)

    offs = sorted(range(1, nz), key=lambda o: -min(o, nz - o))
    for k, off in enumerate(offs):
        owner = lax.rem(mes[0] + off, nz)
        render(owner, tiles.at[k])
        owner_copy(k, owner).start()
    render(mes[0], recv.at[mes[0]])

    for off in offs:
        src = lax.rem(mes[0] + nz - off, nz)
        pltpu.make_async_remote_copy(
            src_ref=tiles.at[0], dst_ref=recv.at[src], send_sem=tile_send.at[0], recv_sem=tile_recv.at[src],
            device_id={"gz": src}, device_id_type=MESH,
        ).wait_recv()

    def composite(i, carry):
        at = pl.ds(pl.multiple_of(8 * i, 8), 8)
        acc = [recv[0, k, at, :] for k in range(4)]
        for s in range(1, nz):
            clear = 1.0 - acc[3]
            acc = [acc[k] + clear * recv[s, k, at, :] for k in range(4)]
        for k in range(4):
            for r in range(8):
                pic_out[0, 0, 8 * i + r, pl.ds(k, 1), :] = acc[k][r : r + 1, :]
        return carry

    lax.fori_loop(0, per_owner // 8, composite, 0)
    for k, off in enumerate(offs):
        owner_copy(k, lax.rem(mes[0] + off, nz)).wait_send()
    for face, _ in waits:
        face.wait_send()
    store.wait()


def shards(fields, diffusivity, courant, tf_center, tf_sharp, tf_gain, tf_color, tile_mask, tile_perm):
    nz = lax.axis_size("gz")
    per_owner = TILES // nz
    f32 = jnp.float32
    smem = pl.BlockSpec(memory_space=pltpu.SMEM)
    vm = pltpu.VMEM
    halo = lambda n: [vm((2, n, CZ, CX), f32), vm((2, n, CZ, CX), f32), vm((2, n, 8, CX), f32), vm((2, n, 8, CX), f32)]
    return pl.pallas_call(
        kernel,
        out_shape=(
            jax.ShapeDtypeStruct((NF, CZ, CY, CX), f32),
            jax.ShapeDtypeStruct((1, 1, per_owner, 4, CX), f32),
        ),
        in_specs=[pl.BlockSpec(memory_space=pl.ANY)] * 2 + [smem] * 7,
        out_specs=(pl.BlockSpec(memory_space=pl.ANY), pl.BlockSpec(memory_space=pltpu.VMEM)),
        scratch_shapes=[
            vm((NF + 1, CZ + 2, 32, CX), f32),
            vm((NF, CZ + 2, 32, CX), f32),
            vm((NF, CZ, CY, CX), f32),
            vm((CZ + 2, 32, CX), f32),
            *halo(NF + 1), *halo(NF), *halo(1),
            vm((CY, CZ, CX), f32),
            vm((CY, CZ, CX), f32),
            vm((3, CY, CZ, CX), f32),
            vm((max(nz - 1, 1), 4, per_owner, CX), f32),
            vm((nz, 4, per_owner, CX), f32),
            pltpu.SemaphoreType.DMA((20,)),
            pltpu.SemaphoreType.DMA((20,)),
            pltpu.SemaphoreType.DMA((nz,)),
            pltpu.SemaphoreType.DMA((nz,)),
            pltpu.SemaphoreType.DMA((3,)),
        ],
        compiler_params=pltpu.CompilerParams(collective_id=0, has_side_effects=True),
        name="insitu",
    )(fields, diffusivity, courant, tf_center, tf_sharp, tf_gain, tf_color, tile_mask, tile_perm)


def solution(mesh):
    return jax.shard_map(
        shards,
        mesh=mesh,
        in_specs=(
            P(None, "gz", "gy", "gx"),
            P("gz", "gy", "gx"),
            P(),
            P(),
            P(),
            P(),
            P(),
            P("gz", None, "gy", "gx"),
            P("gy", "gx", None),
        ),
        out_specs=(P(None, "gz", "gy", "gx"), P("gy", "gx", "gz", None, None)),
        check_vma=False,
    )
```

time: 249 us -> 60.6 us (0.24)
  the two profiles are of different devices: /device:TPU:26 before, /device:TPU:1 now
where the time goes in v1:
time: 60.6 us; the launch traced here: 60.4 us
  Pallas kernels  53.7 us (89%)
  local copies, waits for them, and re-layouts  6.04 us (10%)
  between operations  0.65 us (1%)
    pallas_call x1, Pallas kernels, shards(): pl.pallas_call(kernel, out_shape=(jax.ShapeDtypeStruct((NF, CZ, CY, CX),...  53.7 us
    unnamed x6, local copies, waits for them, and re-layouts  6.04 us

profile of v1, /device:TPU:1, one launch (start us, length us, event | category | flops | bytes accessed | tf_op | source)
XLA Modules:
  0.0 60.4 jit_solution(745945939147088396)
XLA Ops:
  0.6 1.4 %copy.11.courant = f32[5,3]{1,0:T(8,128)} copy(f32[5,3]{0,1:T(4,128)} %param.11) | data formatting | bytes 120 | tf_op args[2]
  2.0 1.5 %copy.12.mask = s32[1,16,16,1]{3,2,1,0:T(8,128)} copy(s32[1,16,16,1]{2,3,1,0:T(1,128)} %param.16) | data formatting | bytes 2048 | tf_op args[7]
  3.5 53.7 %insitu.1 = (f32[5,32,16,128]{3,2,1,0:T(8,128)}, f32[1,1,32,4,128]{4,3,2,1,0:T(4,128)}) custom-call(f32[5,32,16,128]{3,2,1,0:T(8,128)} %fields.1, f32[32,16,128]{2,1,0:T(8,128)} %kappa.1, f32[5,3]{1,0:T(8,128)} %copy.11.courant, f32[16]{0:T(128)} %center.1, f32[16]{0:T(128)} %sharp.1, f32[16]{0:T(128)} %gain.1, f32[3,16]{1,0:T(4,128)} %color.1, ...), custom_call_target="tpu_custom_call" | custom-call | tf_op jit(solution)/shard_map/insitu/pallas_call | solution.py:376
  57.2 0.0 copy-start
  57.2 2.5 %copy.15 = f32[5,32,16,128]{3,2,1,0:T(8,128)} copy(f32[5,32,16,128]{3,2,1,0:T(8,128)} %get-tuple-element.4) | data formatting | bytes 2621440
  59.8 0.0 copy-done
  59.8 0.6 %copy.16 = f32[1,1,32,4,128]{4,3,2,1,0:T(4,128)} copy(f32[1,1,32,4,128]{4,3,2,1,0:T(4,128)S(1)} %copy-done) | data formatting | bytes 131072
Async XLA Ops:
  57.2 2.6 %copy-start = (f32[1,1,32,4,128]{4,3,2,1,0:T(4,128)S(1)}, f32[1,1,32,4,128]{4,3,2,1,0:T(4,128)}, u32[]{:S(2)}) copy-start(f32[1,1,32,4,128]{4,3,2,1,0:T(4,128)} %get-tuple-element.5) | copy-start | bytes 196612

commit v2 on v0

v2 whole, which is shorter than its diff:
```python
import functools
import math

import jax
import jax.numpy as jnp
from jax import lax
from jax.experimental import pallas as pl
from jax.experimental.pallas import tpu as pltpu
from jax.sharding import PartitionSpec as P

MESH = pl.DeviceIdType.MESH
LOG2E = math.log2(math.e)
NF, CZ, CY, CX, TF = 5, 32, 16, 128, 16
R0 = 8
TILES = TF * CY
GROUPS1 = ((0, 2), (2, 3))
GROUPS2 = ((0, 1), (1, 2), (3, 2))
UNROLL = 8


def kernel(
    fields, kappa, courant_in, center_in, sharp_in, gain_in, color_in, mask_in, perm_in,
    u2, pic_out,
    kb, u0, u1, sp, ysendk, yhalok, xsendk, xhalok, ysend1, yhalo1, xsend1, xhalo1,
    ysend2, yhalo2, xsend2, xhalo2, ysend3, yhalo3, xsend3, xhalo3,
    kz, kf, sig, rs, rm, rb, tiles, recv,
    courant, center, sharp, gain, color, mask, perm,
    send_sem, recv_sem, tile_send, tile_recv, local_sem, token,
):
    f32 = jnp.float32
    names = ("gz", "gy", "gx")
    sizes = [lax.axis_size(a) for a in names]
    mes = [lax.axis_index(a) for a in names]
    nz = sizes[0]
    per_owner = TILES // nz
    rows = pl.ds(R0, CY)

    def local(i, src, dst):
        copy = pltpu.make_async_copy(src, dst, local_sem.at[i])
        copy.start()
        return copy

    load_k = local(0, kappa, kb.at[pl.ds(1, CZ), rows, :])
    loads = [local(1 + f, fields.at[f], u0.at[f, pl.ds(1, CZ), rows, :]) for f in range(NF)]
    small = [
        local(6 + i, a, b)
        for i, (a, b) in enumerate(
            zip(
                (courant_in, center_in, sharp_in, gain_in, color_in, mask_in, perm_in),
                (courant, center, sharp, gain, color, mask, perm),
            )
        )
    ]

    def exists(a, side):
        return (mes[a] > 0) if side == 0 else (mes[a] < sizes[a] - 1)

    ring = [lax.rem(mes[0] + 1, nz), lax.rem(mes[0] + nz - 1, nz)]
    barrier = pltpu.get_barrier_semaphore()

    def greet(sem):
        for z in ring:
            pl.semaphore_signal(sem, inc=1, device_id={"gz": z}, device_id_type=MESH)

    greet(barrier)
    count = jnp.int32(2)
    for a in (1, 2):
        for side in (0, 1):
            ok = exists(a, side)

            @pl.when(ok)
            def _(a=a, side=side):
                pl.semaphore_signal(
                    barrier, inc=1, device_id={names[a]: mes[a] + 2 * side - 1}, device_id_type=MESH
                )

            count = count + ok.astype(jnp.int32)

    lane = lax.broadcasted_iota(jnp.int32, (8, 128), 1)
    sub = lax.broadcasted_iota(jnp.int32, (8, 128), 0)
    pair = lax.bitwise_and(lax.shift_right_logical(lane + 1, 1), 63)
    even = lax.bitwise_and(lane, 1) == 0
    first_lane, last_lane = lane == 0, lane == CX - 1
    first_row, last_row = sub == 0, sub == 7
    blank = jnp.zeros((8, 128), f32)

    def rolled(x, shift):
        return pltpu.roll(x, shift, 1)

    def packed(value, into, v):
        return jnp.where(pair == v, rolled(value, 2 * v), into)

    def halo_pack(ref, f):
        return jnp.where(even, rolled(ref[0, f], 1), rolled(ref[1, f], CX - 1))

    for a, side, refs in (
        (0, 0, (kb.at[0, rows, :], u0.at[:, 0, rows, :], u1.at[:, 0, rows, :], sp.at[0, rows, :])),
        (0, 1, (kb.at[CZ + 1, rows, :], u0.at[:, CZ + 1, rows, :], u1.at[:, CZ + 1, rows, :], sp.at[CZ + 1, rows, :])),
        *((1, s, tuple(r.at[s] for r in (yhalok, yhalo1, yhalo2, yhalo3))) for s in (0, 1)),
        *((2, s, tuple(r.at[s] for r in (xhalok, xhalo1, xhalo2, xhalo3))) for s in (0, 1)),
    ):

        @pl.when(jnp.logical_not(exists(a, side)))
        def _(refs=refs):
            for r in refs:
                r[...] = jnp.zeros(r.shape, f32)

    class Faces:
        def __init__(self, sem, parts):
            self.sem, self.parts = sem, parts

        def desc(self, a, side):
            src, dst = self.parts[2 * a + side]
            i = self.sem + 2 * a + side
            return pltpu.make_async_remote_copy(
                src_ref=src, dst_ref=dst, send_sem=send_sem.at[i], recv_sem=recv_sem.at[i],
                device_id={names[a]: mes[a] + 2 * side - 1}, device_id_type=MESH,
            )

        def each(self, what, incoming):
            for a in (1, 2, 0):
                for side in (0, 1):

                    @pl.when(exists(a, 1 - side if incoming else side))
                    def _(a=a, side=side):
                        getattr(self.desc(a, side), what)()

        def start(self):
            self.each("start", False)

        def wait_recv(self):
            self.each("wait_recv", True)

        def wait_send(self):
            self.each("wait_send", False)

    def yx_parts(ys, yh, xs, xh, at):
        return [
            (ys.at[0, at], yh.at[1, at]), (ys.at[1, at], yh.at[0, at]),
            (xs.at[at], xh.at[1, at]), (xs.at[at], xh.at[0, at]),
        ]

    one = pl.ds(0, 1)
    facesk = Faces(0, [
        (kappa.at[0], kb.at[CZ + 1, rows, :]), (kappa.at[CZ - 1], kb.at[0, rows, :]),
        *yx_parts(ysendk, yhalok, xsendk, xhalok, one),
    ])
    faces1, faces2 = [], []
    for g, (f, n) in enumerate(GROUPS1):
        at = pl.ds(f, n)
        faces1.append(Faces(6 + 6 * g, [
            (fields.at[at, 0], u0.at[at, CZ + 1, rows, :]), (fields.at[at, CZ - 1], u0.at[at, 0, rows, :]),
            *yx_parts(ysend1, yhalo1, xsend1, xhalo1, at),
        ]))
    for g, (f, n) in enumerate(GROUPS2):
        at = pl.ds(f, n)
        faces2.append(Faces(18 + 6 * g, [
            (u1.at[at, 1, rows, :], u1.at[at, CZ + 1, rows, :]), (u1.at[at, CZ, rows, :], u1.at[at, 0, rows, :]),
            *yx_parts(ysend2, yhalo2, xsend2, xhalo2, at),
        ]))
    faces3 = Faces(36, [
        (sp.at[1, rows, :], sp.at[CZ + 1, rows, :]), (sp.at[CZ, rows, :], sp.at[0, rows, :]),
        *yx_parts(ysend3, yhalo3, xsend3, xhalo3, one),
    ])

    def sweep(body, init):
        def step(i, carry):
            for j in range(UNROLL):
                carry = body(UNROLL * i + j, carry)
            return carry

        return lax.fori_loop(0, CZ // UNROLL, step, init)

    def pack_planes(ref, ysend, xsend, f):
        def body(z, q):
            ysend[0, f, pl.ds(z, 1), :] = ref[z + 1, pl.ds(R0, 1), :]
            ysend[1, f, pl.ds(z, 1), :] = ref[z + 1, pl.ds(R0 + CY - 1, 1), :]
            for h in range(2):
                q = packed(ref[z + 1, pl.ds(R0 + 8 * h, 8), :], q, 2 * z + h)
            return q

        xsend[f] = sweep(body, blank)

    load_k.wait()
    pack_planes(kb, ysendk, xsendk, 0)
    for f in range(NF):
        loads[f].wait()
        pack_planes(u0.at[f], ysend1, xsend1, f)
    for copy in small:
        copy.wait()
    pl.semaphore_wait(barrier, count)
    facesk.start()
    for face in faces1:
        face.start()
    greet(token.at[0])

    def sides(ref, z, h, yhalo, f, pack):
        row = R0 + 8 * h
        mid = ref[z + 1, pl.ds(row, 8), :]
        zm, zp = ref[z, pl.ds(row, 8), :], ref[z + 2, pl.ds(row, 8), :]
        ym, yp = ref[z + 1, pl.ds(row - 1, 8), :], ref[z + 1, pl.ds(row + 1, 8), :]
        if h == 0:
            ym = jnp.where(first_row, jnp.broadcast_to(yhalo[0, f, pl.ds(z, 1), :], (8, 128)), ym)
        else:
            yp = jnp.where(last_row, jnp.broadcast_to(yhalo[1, f, pl.ds(z, 1), :], (8, 128)), yp)
        edge = rolled(pack, lax.rem(128 - 2 * (2 * z + h), 128))
        xm = jnp.where(first_lane, edge, rolled(mid, 1))
        xp = jnp.where(last_lane, edge, rolled(mid, CX - 1))
        return mid, zm, zp, ym, yp, xm, xp

    facesk.wait_recv()
    kpack = halo_pack(xhalok, 0)

    def coefficients(z, carry):
        for h in range(2):
            at = pl.ds(8 * h, 8)
            mid, *others = sides(kb, z, h, yhalok, 0, kpack)
            means = [0.5 * (mid + w) for w in others]
            kz[z, at, :] = means[0]
            kz[z + 1, at, :] = means[1]
            for i in range(4):
                kf[i, z, at, :] = means[2 + i]
            kf[4, z, at, :] = 1.0 - ((means[0] + means[1]) + (means[2] + means[3]) + (means[4] + means[5]))
        return carry

    sweep(coefficients, 0)

    def advance(src, f, yhalo, xhalo, emit):
        pack = halo_pack(xhalo, f)
        cz, cy, cx = courant[0, f], courant[1, f], courant[2, f]
        total = cz + cy + cx

        def body(z, q):
            for h in range(2):
                at = pl.ds(8 * h, 8)
                mid, zm, zp, ym, yp, xm, xp = sides(src.at[f], z, h, yhalo, f, pack)
                value = (
                    (kf[4, z, at, :] - total) * mid
                    + (kz[z + 1, at, :] * zp + (kz[z, at, :] + cz) * zm)
                    + (kf[1, z, at, :] * yp + (kf[0, z, at, :] + cy) * ym)
                    + (kf[3, z, at, :] * xp + (kf[2, z, at, :] + cx) * xm)
                )
                emit(z, h, value)
                if q is not None:
                    q = packed(value, q, 2 * z + h)
            return q

        return body

    def step1(f):
        def emit(z, h, value):
            u1[f, z + 1, pl.ds(R0 + 8 * h, 8), :] = value
            side, row = (0, 0) if h == 0 else (1, 7)
            ysend2[side, f, pl.ds(z, 1), :] = value[row : row + 1, :]

        xsend2[f] = sweep(advance(u0, f, yhalo1, xhalo1, emit), blank)

    arrivals1 = {f: faces1[g] for g, (f, n) in enumerate(GROUPS1)}
    departures2 = {f + n - 1: faces2[g] for g, (f, n) in enumerate(GROUPS2)}
    for f in range(NF):
        if f in arrivals1:
            arrivals1[f].wait_recv()
        step1(f)
        if f in departures2:
            departures2[f].start()
    pl.semaphore_wait(token.at[0], 2)
    greet(token.at[1])

    def sites(z, h):
        start = h * 8 * CZ + lax.rem(z, 4) * 8 + lax.div(z, 4)
        return pl.ds(start, 8, stride=CZ)

    rs2, rm2 = rs.reshape(CY * CZ, CX), rm.reshape(CY * CZ, CX)
    rb2 = rb.reshape(3, CY * CZ, CX)

    def step2(f):
        def emit(z, h, value):
            at = pl.ds(8 * h, 8)
            u2[f, z, at, :] = value
            if f == 0:
                sp[z + 1, pl.ds(R0 + 8 * h, 8), :] = value
                side, row = (0, 0) if h == 0 else (1, 7)
                ysend3[side, 0, pl.ds(z, 1), :] = value[row : row + 1, :]
                rs2[sites(z, h), :] = value
            elif f == 4:
                rm2[sites(z, h), :] = (-LOG2E) - (0.5 * LOG2E) * jnp.tanh(value)
            else:
                sig[f - 1, z, at, :] = 0.5 + 0.5 * jnp.tanh(0.5 * value)

        out = sweep(advance(u1, f, yhalo2, xhalo2, emit), blank if f == 0 else None)
        if f == 0:
            xsend3[0] = out

    arrivals2 = {f: faces2[g] for g, (f, n) in enumerate(GROUPS2)}
    for f in range(NF):
        if f in arrivals2:
            arrivals2[f].wait_recv()
        step2(f)
        if f == 0:
            faces3.start()
            pl.semaphore_wait(token.at[1], 2)
            greet(token.at[2])

    faces3.wait_recv()
    spack = halo_pack(xhalo3, 0)

    def shading(z, carry):
        for h in range(2):
            _, zm, zp, ym, yp, xm, xp = sides(sp, z, h, yhalo3, 0, spack)
            gz, gy, gx = 0.5 * (zp - zm), 0.5 * (yp - ym), 0.5 * (xp - xm)
            shade = 0.35 + 0.65 * jnp.abs(0.64 * gz + 0.6 * gy + 0.48 * gx) * lax.rsqrt(
                gz * gz + gy * gy + gx * gx + 1.0
            )
            for k in range(3):
                rb2[k, sites(z, h), :] = shade * sig[k, z, pl.ds(8 * h, 8), :]
        return carry

    sweep(shading, 0)
    pl.semaphore_wait(token.at[2], 2)

    def owner_copy(k, owner):
        return pltpu.make_async_remote_copy(
            src_ref=tiles.at[k], dst_ref=recv.at[mes[0]],
            send_sem=tile_send.at[k], recv_sem=tile_recv.at[mes[0]],
            device_id={"gz": owner}, device_id_type=MESH,
        )

    def render(owner, dst):
        def tile(i, carry):
            p = perm[0, 0, owner * per_owner + i]
            t = lax.shift_right_logical(p, 4)
            y = lax.bitwise_and(p, 15)
            cover = mask[0, t, 0, y].astype(f32)
            mid, slope, amount = center[t], -LOG2E * sharp[t], gain[t]
            gap = rs[y] - mid
            depth = jnp.exp2(slope * (gap * gap)) * (amount * rm[y])
            e = [depth[0:8]]
            for w in range(1, 4):
                e.append(e[-1] + depth[8 * w : 8 * w + 8])
            inclusive = e[3]
            for sh in (1, 2, 4):
                inclusive = inclusive + jnp.where(sub >= sh, pltpu.roll(inclusive, sh, 0), 0.0)
            before = jnp.exp2(inclusive - e[3])
            lit = [jnp.exp2(x) for x in e]
            weight = [1.0 - lit[0]] + [lit[w] - lit[w + 1] for w in range(3)]
            for k in range(3):
                base = rb[k, y]
                total = weight[0] * base[0:8]
                for w in range(1, 4):
                    total = total + weight[w] * base[8 * w : 8 * w + 8]
                total = jnp.sum(total * before, axis=0, keepdims=True)
                dst[k, pl.ds(i, 1), :] = total * (color[k, t] * cover)
            dst[3, pl.ds(i, 1), :] = (1.0 - jnp.exp2(inclusive[7:8])) * cover
            return carry

        lax.fori_loop(0, per_owner, tile, 0, unroll=4)

    offs = sorted(range(1, nz), key=lambda o: -min(o, nz - o))
    for k, off in enumerate(offs):
        owner = lax.rem(mes[0] + off, nz)
        render(owner, tiles.at[k])
        owner_copy(k, owner).start()
    render(mes[0], recv.at[mes[0]])

    for off in offs:
        src = lax.rem(mes[0] + nz - off, nz)
        pltpu.make_async_remote_copy(
            src_ref=tiles.at[0], dst_ref=recv.at[src], send_sem=tile_send.at[0], recv_sem=tile_recv.at[src],
            device_id={"gz": src}, device_id_type=MESH,
        ).wait_recv()

    def composite(i, carry):
        at = pl.ds(pl.multiple_of(8 * i, 8), 8)
        acc = [recv[0, k, at, :] for k in range(4)]
        for s in range(1, nz):
            clear = 1.0 - acc[3]
            acc = [acc[k] + clear * recv[s, k, at, :] for k in range(4)]
        for k in range(4):
            for r in range(8):
                pic_out[0, 0, 8 * i + r, pl.ds(k, 1), :] = acc[k][r : r + 1, :]
        return carry

    lax.fori_loop(0, per_owner // 8, composite, 0)
    for k, off in enumerate(offs):
        owner_copy(k, lax.rem(mes[0] + off, nz)).wait_send()
    for face in [facesk, *faces1, *faces2, faces3]:
        face.wait_send()


def shards(fields, diffusivity, courant, tf_center, tf_sharp, tf_gain, tf_color, tile_mask, tile_perm):
    nz = lax.axis_size("gz")
    per_owner = TILES // nz
    f32 = jnp.float32
    vm = pltpu.VMEM
    anywhere = pl.BlockSpec(memory_space=pl.ANY)
    inside = pl.BlockSpec(memory_space=pltpu.VMEM)

    def halo(n):
        return [vm((2, n, CZ, CX), f32), vm((2, n, CZ, CX), f32), vm((n, 8, CX), f32), vm((2, n, 8, CX), f32)]

    sm = lambda a: pltpu.SMEM(a.shape, a.dtype)
    operands = (
        fields, diffusivity, courant.T, tf_center, tf_sharp, tf_gain, tf_color,
        jnp.transpose(tile_mask, (0, 1, 3, 2)), tile_perm,
    )
    return pl.pallas_call(
        kernel,
        out_shape=(vm((NF, CZ, CY, CX), f32), vm((1, 1, per_owner, 4, CX), f32)),
        in_specs=[anywhere] * 9,
        out_specs=(inside, inside),
        scratch_shapes=[
            vm((CZ + 2, 32, CX), f32),
            vm((NF, CZ + 2, 32, CX), f32),
            vm((NF, CZ + 2, 32, CX), f32),
            vm((CZ + 2, 32, CX), f32),
            *halo(1), *halo(NF), *halo(NF), *halo(1),
            vm((CZ + 1, CY, CX), f32),
            vm((5, CZ, CY, CX), f32),
            vm((3, CZ, CY, CX), f32),
            vm((CY, CZ, CX), f32),
            vm((CY, CZ, CX), f32),
            vm((3, CY, CZ, CX), f32),
            vm((max(nz - 1, 1), 4, per_owner, CX), f32),
            vm((nz, 4, per_owner, CX), f32),
            *[sm(a) for a in operands[2:]],
            pltpu.SemaphoreType.DMA((42,)),
            pltpu.SemaphoreType.DMA((42,)),
            pltpu.SemaphoreType.DMA((nz,)),
            pltpu.SemaphoreType.DMA((nz,)),
            pltpu.SemaphoreType.DMA((13,)),
            pltpu.SemaphoreType.REGULAR((3,)),
        ],
        compiler_params=pltpu.CompilerParams(collective_id=0, has_side_effects=True),
        name="insitu",
    )(*operands)


def solution(mesh):
    return jax.shard_map(
        shards,
        mesh=mesh,
        in_specs=(
            P(None, "gz", "gy", "gx"),
            P("gz", "gy", "gx"),
            P(),
            P(),
            P(),
            P(),
            P(),
            P("gz", None, "gy", "gx"),
            P("gy", "gx", None),
        ),
        out_specs=(P(None, "gz", "gy", "gx"), P("gy", "gx", "gz", None, None)),
        check_vma=False,
    )
```

time: 249 us -> 41.1 us (0.17)
  the two profiles are of different devices: /device:TPU:26 before, /device:TPU:1 now
where the time goes in v2:
time: 41.1 us; the launch traced here: 41 us
  Pallas kernels  38.6 us (94%)
  local copies, waits for them, and re-layouts  1.69 us (4%)
  between operations  0.64 us (2%)
    pallas_call x1, Pallas kernels, shards(): pl.pallas_call(kernel, out_shape=(vm((NF, CZ, CY, CX), f32), vm((1, 1, pe...  38.6 us
    unnamed x2, local copies, waits for them, and re-layouts  1.69 us

profile of v2, /device:TPU:1, one launch (start us, length us, event | category | flops | bytes accessed | tf_op | source)
XLA Modules:
  0.0 41.0 jit_solution(16051612524933558092)
XLA Ops:
  0.6 38.6 %insitu.1 = (f32[5,32,16,128]{3,2,1,0:T(8,128)S(1)}, f32[1,1,32,4,128]{4,3,2,1,0:T(4,128)S(1)}) custom-call(f32[5,32,16,128]{3,2,1,0:T(8,128)} %fields.1, f32[32,16,128]{2,1,0:T(8,128)} %kappa.1, f32[3,5]{1,0:T(4,128)} %bitcast.3, f32[16]{0:T(128)} %center_in.1, f32[16]{0:T(128)} %sharp_in.1, f32[16]{0:T(128)} %gain_in.1, f32[3,16]{1,0:T(4,128)} %color_in.1, ...), custom_call_target="tpu_custom_call" | custom-call | tf_op jit(solution)/shard_map/insitu/pallas_call | solution.py:406
  39.3 1.1 %copy.13 = f32[5,32,16,128]{3,2,1,0:T(8,128)} copy(f32[5,32,16,128]{3,2,1,0:T(8,128)S(1)} %get-tuple-element.2) | data formatting | bytes 2621440
  40.3 0.6 %copy.14 = f32[1,1,32,4,128]{4,3,2,1,0:T(4,128)} copy(f32[1,1,32,4,128]{4,3,2,1,0:T(4,128)S(1)} %get-tuple-element.3) | data formatting | bytes 131072

commit v3 on v2

--- a/solution.py
+++ b/solution.py
@@ -15,7 +15,7 @@
 TILES = TF * CY
 GROUPS1 = ((0, 2), (2, 3))
 GROUPS2 = ((0, 1), (1, 2), (3, 2))
-UNROLL = 8
+UNROLL = 16
 
 
 def kernel(
@@ -23,7 +23,7 @@
     u2, pic_out,
     kb, u0, u1, sp, ysendk, yhalok, xsendk, xhalok, ysend1, yhalo1, xsend1, xhalo1,
     ysend2, yhalo2, xsend2, xhalo2, ysend3, yhalo3, xsend3, xhalo3,
-    kz, kf, sig, rs, rm, rb, tiles, recv,
+    kz, kf, rs, rm, rh, rb, mtiles, mrecv, rtiles, ptiles, precv, recv,
     courant, center, sharp, gain, color, mask, perm,
     send_sem, recv_sem, tile_send, tile_recv, local_sem, token,
 ):
@@ -271,7 +271,7 @@
         return pl.ds(start, 8, stride=CZ)
 
     rs2, rm2 = rs.reshape(CY * CZ, CX), rm.reshape(CY * CZ, CX)
-    rb2 = rb.reshape(3, CY * CZ, CX)
+    rh2, rb2 = rh.reshape(CY * CZ, CX), rb.reshape(3, CY * CZ, CX)
 
     def step2(f):
         def emit(z, h, value):
@@ -285,7 +285,7 @@
             elif f == 4:
                 rm2[sites(z, h), :] = (-LOG2E) - (0.5 * LOG2E) * jnp.tanh(value)
             else:
-                sig[f - 1, z, at, :] = 0.5 + 0.5 * jnp.tanh(0.5 * value)
+                rb2[f - 1, sites(z, h), :] = 0.5 + 0.5 * jnp.tanh(0.5 * value)
 
         out = sweep(advance(u1, f, yhalo2, xhalo2, emit), blank if f == 0 else None)
         if f == 0:
@@ -298,8 +298,6 @@
         step2(f)
         if f == 0:
             faces3.start()
-            pl.semaphore_wait(token.at[1], 2)
-            greet(token.at[2])
 
     faces3.wait_recv()
     spack = halo_pack(xhalo3, 0)
@@ -311,18 +309,25 @@
             shade = 0.35 + 0.65 * jnp.abs(0.64 * gz + 0.6 * gy + 0.48 * gx) * lax.rsqrt(
                 gz * gz + gy * gy + gx * gx + 1.0
             )
-            for k in range(3):
-                rb2[k, sites(z, h), :] = shade * sig[k, z, pl.ds(8 * h, 8), :]
+            rh2[sites(z, h), :] = shade
         return carry
 
     sweep(shading, 0)
-    pl.semaphore_wait(token.at[2], 2)
-
-    def owner_copy(k, owner):
+    pl.semaphore_wait(token.at[1], 2)
+
+    pairs, relays = nz // 2, nz // 2 - 1
+    odd = lax.rem(mes[0], 2)
+    ahead = 2 * odd - 1
+    mate = mes[0] - ahead
+    mine = lax.div(mes[0], 2)
+
+    def at_distance(start, d):
+        return lax.rem(start + d * ahead + nz, nz)
+
+    def block_copy(i, src, dst, z):
         return pltpu.make_async_remote_copy(
-            src_ref=tiles.at[k], dst_ref=recv.at[mes[0]],
-            send_sem=tile_send.at[k], recv_sem=tile_recv.at[mes[0]],
-            device_id={"gz": owner}, device_id_type=MESH,
+            src_ref=src, dst_ref=dst, send_sem=tile_send.at[i], recv_sem=tile_recv.at[i],
+            device_id={"gz": z}, device_id_type=MESH,
         )
 
     def render(owner, dst):
@@ -343,6 +348,8 @@
             before = jnp.exp2(inclusive - e[3])
             lit = [jnp.exp2(x) for x in e]
             weight = [1.0 - lit[0]] + [lit[w] - lit[w + 1] for w in range(3)]
+            shade = rh[y]
+            weight = [weight[w] * shade[8 * w : 8 * w + 8] for w in range(4)]
             for k in range(3):
                 base = rb[k, y]
                 total = weight[0] * base[0:8]
@@ -353,26 +360,61 @@
             dst[3, pl.ds(i, 1), :] = (1.0 - jnp.exp2(inclusive[7:8])) * cover
             return carry
 
-        lax.fori_loop(0, per_owner, tile, 0, unroll=4)
-
-    offs = sorted(range(1, nz), key=lambda o: -min(o, nz - o))
-    for k, off in enumerate(offs):
-        owner = lax.rem(mes[0] + off, nz)
-        render(owner, tiles.at[k])
-        owner_copy(k, owner).start()
-    render(mes[0], recv.at[mes[0]])
-
-    for off in offs:
-        src = lax.rem(mes[0] + nz - off, nz)
+        lax.fori_loop(0, per_owner, tile, 0, unroll=8)
+
+    def merge(theirs, own):
+        for i in range(per_owner // 8):
+            at = pl.ds(8 * i, 8)
+            a = [theirs[k, at, :] for k in range(4)]
+            b = [own[k, at, :] for k in range(4)]
+            front = [jnp.where(odd == 1, x, y) for x, y in zip(a, b)]
+            back = [jnp.where(odd == 1, y, x) for x, y in zip(a, b)]
+            clear = 1.0 - front[3]
+            for k in range(4):
+                own[k, at, :] = front[k] + clear * back[k]
+
+    def to_mate(d):
+        return block_copy(pairs + d, mtiles.at[d - 1], mrecv.at[d - 1], mate)
+
+    def onward(d):
+        return pltpu.make_async_remote_copy(
+            src_ref=rtiles.at[d - 1], dst_ref=recv.at[mine],
+            send_sem=tile_send.at[d - 1], recv_sem=tile_recv.at[mine],
+            device_id={"gz": at_distance(mes[0], d)}, device_id_type=MESH,
+        )
+
+    def pass_on(d):
+        to_mate(d).wait_recv()
+        merge(mrecv.at[d - 1], rtiles.at[d - 1])
+        onward(d).start()
+
+    order = list(range(relays, 0, -1))
+    for d in order:
+        render(at_distance(mate, -d), mtiles.at[d - 1])
+        to_mate(d).start()
+    pair_copy = block_copy(pairs, ptiles, precv, mate)
+    for j, d in enumerate(order):
+        render(at_distance(mes[0], d), rtiles.at[d - 1])
+        if j:
+            pass_on(order[j - 1])
+    render(mate, ptiles)
+    pair_copy.start()
+    if order:
+        pass_on(order[-1])
+    render(mes[0], recv.at[mine])
+    pair_copy.wait_recv()
+    merge(precv, recv.at[mine])
+    for o in range(1, pairs):
+        q = lax.rem(mine + o, pairs)
         pltpu.make_async_remote_copy(
-            src_ref=tiles.at[0], dst_ref=recv.at[src], send_sem=tile_send.at[0], recv_sem=tile_recv.at[src],
-            device_id={"gz": src}, device_id_type=MESH,
+            src_ref=rtiles.at[0], dst_ref=recv.at[q], send_sem=tile_send.at[0], recv_sem=tile_recv.at[q],
+            device_id={"gz": mate}, device_id_type=MESH,
         ).wait_recv()
 
     def composite(i, carry):
         at = pl.ds(pl.multiple_of(8 * i, 8), 8)
         acc = [recv[0, k, at, :] for k in range(4)]
-        for s in range(1, nz):
+        for s in range(1, pairs):
             clear = 1.0 - acc[3]
             acc = [acc[k] + clear * recv[s, k, at, :] for k in range(4)]
         for k in range(4):
@@ -381,10 +423,21 @@
         return carry
 
     lax.fori_loop(0, per_owner // 8, composite, 0)
-    for k, off in enumerate(offs):
-        owner_copy(k, lax.rem(mes[0] + off, nz)).wait_send()
+    for d in order:
+        to_mate(d).wait_send()
+        onward(d).wait_send()
+    pair_copy.wait_send()
     for face in [facesk, *faces1, *faces2, faces3]:
         face.wait_send()
+
+
+def flush(state, picture, state_out, picture_out, sem):
+    copies = [pltpu.make_async_copy(picture, picture_out, sem.at[NF])]
+    copies += [pltpu.make_async_copy(state.at[f], state_out.at[f], sem.at[f]) for f in range(NF)]
+    for copy in copies:
+        copy.start()
+    for copy in copies:
+        copy.wait()
 
 
 def shards(fields, diffusivity, courant, tf_center, tf_sharp, tf_gain, tf_color, tile_mask, tile_perm):
@@ -403,7 +456,7 @@
         fields, diffusivity, courant.T, tf_center, tf_sharp, tf_gain, tf_color,
         jnp.transpose(tile_mask, (0, 1, 3, 2)), tile_perm,
     )
-    return pl.pallas_call(
+    results = pl.pallas_call(
         kernel,
         out_shape=(vm((NF, CZ, CY, CX), f32), vm((1, 1, per_owner, 4, CX), f32)),
         in_specs=[anywhere] * 9,
@@ -416,23 +469,32 @@
             *halo(1), *halo(NF), *halo(NF), *halo(1),
             vm((CZ + 1, CY, CX), f32),
             vm((5, CZ, CY, CX), f32),
-            vm((3, CZ, CY, CX), f32),
+            vm((CY, CZ, CX), f32),
             vm((CY, CZ, CX), f32),
             vm((CY, CZ, CX), f32),
             vm((3, CY, CZ, CX), f32),
-            vm((max(nz - 1, 1), 4, per_owner, CX), f32),
-            vm((nz, 4, per_owner, CX), f32),
+            *[vm((max(nz // 2 - 1, 1), 4, per_owner, CX), f32)] * 3,
+            *[vm((4, per_owner, CX), f32)] * 2,
+            vm((nz // 2, 4, per_owner, CX), f32),
             *[sm(a) for a in operands[2:]],
             pltpu.SemaphoreType.DMA((42,)),
             pltpu.SemaphoreType.DMA((42,)),
             pltpu.SemaphoreType.DMA((nz,)),
             pltpu.SemaphoreType.DMA((nz,)),
             pltpu.SemaphoreType.DMA((13,)),
-            pltpu.SemaphoreType.REGULAR((3,)),
+            pltpu.SemaphoreType.REGULAR((2,)),
         ],
         compiler_params=pltpu.CompilerParams(collective_id=0, has_side_effects=True),
         name="insitu",
     )(*operands)
+    return pl.pallas_call(
+        flush,
+        out_shape=tuple(jax.ShapeDtypeStruct(r.shape, f32) for r in results),
+        in_specs=[inside] * 2,
+        out_specs=(anywhere, anywhere),
+        scratch_shapes=[pltpu.SemaphoreType.DMA((NF + 1,))],
+        name="flush",
+    )(*[pltpu.with_memory_space_constraint(r, pltpu.VMEM) for r in results])
 
 
 def solution(mesh):

time: 41.1 us -> 34.2 us (0.83)
  Pallas kernels: 38.6 us -> 33.5 us
  local copies, waits for them, and re-layouts: 1.69 us -> 0 us
    pallas_call x1, Pallas kernels: 38.6 us -> 32.3 us  [shards(): pl.pallas_call(kernel, out_shape=(vm((NF, CZ, CY, CX), f32), vm((1, 1, pe...]
    unnamed x2 -> x0, local copies, waits for them, and re-layouts: 1.69 us -> none
    pallas_call x0 -> x1, Pallas kernels: none -> 1.12 us  [shards(): pl.pallas_call(flush, out_shape=tuple((jax.ShapeDtypeStruct(r.shape, f32)...]
where the time goes in v3:
time: 34.2 us; the launch traced here: 34.1 us
  Pallas kernels  33.5 us (98%)
  between operations  0.64 us (2%)
    pallas_call x1, Pallas kernels, shards(): pl.pallas_call(kernel, out_shape=(vm((NF, CZ, CY, CX), f32), vm((1, 1, pe...  32.3 us
    pallas_call x1, Pallas kernels, shards(): pl.pallas_call(flush, out_shape=tuple((jax.ShapeDtypeStruct(r.shape, f32)...  1.12 us

profile of v3, /device:TPU:1, one launch (start us, length us, event | category | flops | bytes accessed | tf_op | source)
XLA Modules:
  0.0 34.1 jit_solution(9158186585679632051)
XLA Ops:
  0.6 32.3 %insitu.1 = (f32[5,32,16,128]{3,2,1,0:T(8,128)S(1)}, f32[1,1,32,4,128]{4,3,2,1,0:T(4,128)S(1)}) custom-call(f32[5,32,16,128]{3,2,1,0:T(8,128)} %fields.1, f32[32,16,128]{2,1,0:T(8,128)} %kappa.1, f32[3,5]{1,0:T(4,128)} %bitcast.3, f32[16]{0:T(128)} %center_in.1, f32[16]{0:T(128)} %sharp_in.1, f32[16]{0:T(128)} %gain_in.1, f32[3,16]{1,0:T(4,128)} %color_in.1, ...), custom_call_target="tpu_custom_call" | custom-call | tf_op jit(solution)/shard_map/insitu/pallas_call | solution.py:459
  33.0 1.1 %flush.1 = (f32[5,32,16,128]{3,2,1,0:T(8,128)}, f32[1,1,32,4,128]{4,3,2,1,0:T(4,128)}) custom-call(f32[5,32,16,128]{3,2,1,0:T(8,128)S(1)} %get-tuple-element.4.state, f32[1,1,32,4,128]{4,3,2,1,0:T(4,128)S(1)} %get-tuple-element.5.picture), custom_call_target="tpu_custom_call" | custom-call | tf_op jit(solution)/shard_map/flush/pallas_call | solution.py:490

commit v4 on v3

--- a/solution.py
+++ b/solution.py
@@ -15,7 +15,7 @@
 TILES = TF * CY
 GROUPS1 = ((0, 2), (2, 3))
 GROUPS2 = ((0, 1), (1, 2), (3, 2))
-UNROLL = 16
+UNROLL = 32
 
 
 def kernel(
@@ -186,8 +186,6 @@
     for f in range(NF):
         loads[f].wait()
         pack_planes(u0.at[f], ysend1, xsend1, f)
-    for copy in small:
-        copy.wait()
     pl.semaphore_wait(barrier, count)
     facesk.start()
     for face in faces1:
@@ -255,6 +253,7 @@
 
         xsend2[f] = sweep(advance(u0, f, yhalo1, xhalo1, emit), blank)
 
+    small[0].wait()
     arrivals1 = {f: faces1[g] for g, (f, n) in enumerate(GROUPS1)}
     departures2 = {f + n - 1: faces2[g] for g, (f, n) in enumerate(GROUPS2)}
     for f in range(NF):
@@ -313,6 +312,8 @@
         return carry
 
     sweep(shading, 0)
+    for copy in small[1:]:
+        copy.wait()
     pl.semaphore_wait(token.at[1], 2)
 
     pairs, relays = nz // 2, nz // 2 - 1
@@ -330,37 +331,56 @@
             device_id={"gz": z}, device_id_type=MESH,
         )
 
+    def gather_rows(x):
+        low, mid, bit = sub < 4, lax.bitwise_and(sub, 2) == 0, lax.bitwise_and(sub, 1) == 0
+        x = [
+            jnp.where(low, x[i], x[i + 4]) + pltpu.roll(jnp.where(low, x[i + 4], x[i]), 4, 0)
+            for i in range(4)
+        ]
+        for mask_, step in ((mid, 2), (bit, 1)):
+            x = [
+                jnp.where(
+                    mask_, x[i] + pltpu.roll(x[i], 8 - step, 0), x[i + step] + pltpu.roll(x[i + step], step, 0)
+                )
+                for i in range(step)
+            ]
+        return x[0]
+
     def render(owner, dst):
-        def tile(i, carry):
-            p = perm[0, 0, owner * per_owner + i]
-            t = lax.shift_right_logical(p, 4)
-            y = lax.bitwise_and(p, 15)
-            cover = mask[0, t, 0, y].astype(f32)
-            mid, slope, amount = center[t], -LOG2E * sharp[t], gain[t]
-            gap = rs[y] - mid
-            depth = jnp.exp2(slope * (gap * gap)) * (amount * rm[y])
-            e = [depth[0:8]]
-            for w in range(1, 4):
-                e.append(e[-1] + depth[8 * w : 8 * w + 8])
-            inclusive = e[3]
-            for sh in (1, 2, 4):
-                inclusive = inclusive + jnp.where(sub >= sh, pltpu.roll(inclusive, sh, 0), 0.0)
-            before = jnp.exp2(inclusive - e[3])
-            lit = [jnp.exp2(x) for x in e]
-            weight = [1.0 - lit[0]] + [lit[w] - lit[w + 1] for w in range(3)]
-            shade = rh[y]
-            weight = [weight[w] * shade[8 * w : 8 * w + 8] for w in range(4)]
+        def eight(i8, carry):
+            sums = [[], [], []]
+            for j in range(8):
+                i = 8 * i8 + j
+                p = perm[0, 0, owner * per_owner + i]
+                t = lax.shift_right_logical(p, 4)
+                y = lax.bitwise_and(p, 15)
+                cover = mask[0, t, 0, y].astype(f32)
+                mid, slope, amount = center[t], -LOG2E * sharp[t], gain[t]
+                gap = rs[y] - mid
+                depth = jnp.exp2(slope * (gap * gap)) * (amount * rm[y])
+                e = [depth[0:8]]
+                for w in range(1, 4):
+                    e.append(e[-1] + depth[8 * w : 8 * w + 8])
+                inclusive = e[3]
+                for sh in (1, 2, 4):
+                    inclusive = inclusive + jnp.where(sub >= sh, pltpu.roll(inclusive, sh, 0), 0.0)
+                before = jnp.exp2(inclusive - e[3])
+                lit = [jnp.exp2(x) for x in e]
+                weight = [1.0 - lit[0]] + [lit[w] - lit[w + 1] for w in range(3)]
+                shade = rh[y]
+                weight = [weight[w] * shade[8 * w : 8 * w + 8] for w in range(4)]
+                for k in range(3):
+                    base = rb[k, y]
+                    total = weight[0] * base[0:8]
+                    for w in range(1, 4):
+                        total = total + weight[w] * base[8 * w : 8 * w + 8]
+                    sums[k].append((total * before) * (color[k, t] * cover))
+                dst[3, pl.ds(i, 1), :] = (1.0 - jnp.exp2(inclusive[7:8])) * cover
             for k in range(3):
-                base = rb[k, y]
-                total = weight[0] * base[0:8]
-                for w in range(1, 4):
-                    total = total + weight[w] * base[8 * w : 8 * w + 8]
-                total = jnp.sum(total * before, axis=0, keepdims=True)
-                dst[k, pl.ds(i, 1), :] = total * (color[k, t] * cover)
-            dst[3, pl.ds(i, 1), :] = (1.0 - jnp.exp2(inclusive[7:8])) * cover
+                dst[k, pl.ds(pl.multiple_of(8 * i8, 8), 8), :] = gather_rows(sums[k])
             return carry
 
-        lax.fori_loop(0, per_owner, tile, 0, unroll=8)
+        lax.fori_loop(0, per_owner // 8, eight, 0)
 
     def merge(theirs, own):
         for i in range(per_owner // 8):

time: 34.2 us -> 39.4 us (1.15)
  Pallas kernels: 33.5 us -> 38.5 us
    pallas_call x1, Pallas kernels: 32.3 us -> 37.4 us  [shards(): pl.pallas_call(kernel, out_shape=(vm((NF, CZ, CY, CX), f32), vm((1, 1, pe...]
where the time goes in v4:
time: 39.4 us; the launch traced here: 39.2 us
  Pallas kernels  38.5 us (98%)
  between operations  0.64 us (2%)
    pallas_call x1, Pallas kernels, shards(): pl.pallas_call(kernel, out_shape=(vm((NF, CZ, CY, CX), f32), vm((1, 1, pe...  37.4 us
    pallas_call x1, Pallas kernels, shards(): pl.pallas_call(flush, out_shape=tuple((jax.ShapeDtypeStruct(r.shape, f32)...  1.12 us

profile of v4, /device:TPU:1, one launch (start us, length us, event | category | flops | bytes accessed | tf_op | source)
XLA Modules:
  0.0 39.2 jit_solution(15097429021101190474)
XLA Ops:
  0.6 37.4 %insitu.1 = (f32[5,32,16,128]{3,2,1,0:T(8,128)S(1)}, f32[1,1,32,4,128]{4,3,2,1,0:T(4,128)S(1)}) custom-call(f32[5,32,16,128]{3,2,1,0:T(8,128)} %fields.1, f32[32,16,128]{2,1,0:T(8,128)} %kappa.1, f32[3,5]{1,0:T(4,128)} %bitcast.3, f32[16]{0:T(128)} %center_in.1, f32[16]{0:T(128)} %sharp_in.1, f32[16]{0:T(128)} %gain_in.1, f32[3,16]{1,0:T(4,128)} %color_in.1, ...), custom_call_target="tpu_custom_call" | custom-call | tf_op jit(solution)/shard_map/insitu/pallas_call | solution.py:479
  38.0 1.1 %flush.1 = (f32[5,32,16,128]{3,2,1,0:T(8,128)}, f32[1,1,32,4,128]{4,3,2,1,0:T(4,128)}) custom-call(f32[5,32,16,128]{3,2,1,0:T(8,128)S(1)} %get-tuple-element.4.state, f32[1,1,32,4,128]{4,3,2,1,0:T(4,128)S(1)} %get-tuple-element.5.picture), custom_call_target="tpu_custom_call" | custom-call | tf_op jit(solution)/shard_map/flush/pallas_call | solution.py:510

commit v5 on v4

--- a/solution.py
+++ b/solution.py
@@ -15,15 +15,15 @@
 TILES = TF * CY
 GROUPS1 = ((0, 2), (2, 3))
 GROUPS2 = ((0, 1), (1, 2), (3, 2))
-UNROLL = 32
+UNROLL = 16
 
 
 def kernel(
     fields, kappa, courant_in, center_in, sharp_in, gain_in, color_in, mask_in, perm_in,
     u2, pic_out,
-    kb, u0, u1, sp, ysendk, yhalok, xsendk, xhalok, ysend1, yhalo1, xsend1, xhalo1,
+    u0, u1, sp, ysend1, yhalo1, xsend1, xhalo1,
     ysend2, yhalo2, xsend2, xhalo2, ysend3, yhalo3, xsend3, xhalo3,
-    kz, kf, rs, rm, rh, rb, mtiles, mrecv, rtiles, ptiles, precv, recv,
+    kz, kf, rs, rh, rb, blocks, mrecv, precv, recv,
     courant, center, sharp, gain, color, mask, perm,
     send_sem, recv_sem, tile_send, tile_recv, local_sem, token,
 ):
@@ -40,10 +40,14 @@
         copy.start()
         return copy
 
-    load_k = local(0, kappa, kb.at[pl.ds(1, CZ), rows, :])
-    loads = [local(1 + f, fields.at[f], u0.at[f, pl.ds(1, CZ), rows, :]) for f in range(NF)]
+    def load(f):
+        return pltpu.make_async_copy(fields.at[f], u0.at[f, pl.ds(1, CZ), rows, :], local_sem.at[f])
+
+    load_k = local(NF, kappa, u0.at[NF, pl.ds(1, CZ), rows, :])
+    for f in range(NF):
+        load(f).start()
     small = [
-        local(6 + i, a, b)
+        local(NF + 1 + i, a, b)
         for i, (a, b) in enumerate(
             zip(
                 (courant_in, center_in, sharp_in, gain_in, color_in, mask_in, perm_in),
@@ -94,10 +98,10 @@
         return jnp.where(even, rolled(ref[0, f], 1), rolled(ref[1, f], CX - 1))
 
     for a, side, refs in (
-        (0, 0, (kb.at[0, rows, :], u0.at[:, 0, rows, :], u1.at[:, 0, rows, :], sp.at[0, rows, :])),
-        (0, 1, (kb.at[CZ + 1, rows, :], u0.at[:, CZ + 1, rows, :], u1.at[:, CZ + 1, rows, :], sp.at[CZ + 1, rows, :])),
-        *((1, s, tuple(r.at[s] for r in (yhalok, yhalo1, yhalo2, yhalo3))) for s in (0, 1)),
-        *((2, s, tuple(r.at[s] for r in (xhalok, xhalo1, xhalo2, xhalo3))) for s in (0, 1)),
+        (0, 0, (u0.at[:, 0, rows, :], u1.at[:, 0, rows, :], sp.at[0, rows, :])),
+        (0, 1, (u0.at[:, CZ + 1, rows, :], u1.at[:, CZ + 1, rows, :], sp.at[CZ + 1, rows, :])),
+        *((1, s, tuple(r.at[s] for r in (yhalo1, yhalo2, yhalo3))) for s in (0, 1)),
+        *((2, s, tuple(r.at[s] for r in (xhalo1, xhalo2, xhalo3))) for s in (0, 1)),
     ):
 
         @pl.when(jnp.logical_not(exists(a, side)))
@@ -117,22 +121,14 @@
                 device_id={names[a]: mes[a] + 2 * side - 1}, device_id_type=MESH,
             )
 
-        def each(self, what, incoming):
-            for a in (1, 2, 0):
-                for side in (0, 1):
-
-                    @pl.when(exists(a, 1 - side if incoming else side))
-                    def _(a=a, side=side):
-                        getattr(self.desc(a, side), what)()
-
-        def start(self):
-            self.each("start", False)
-
-        def wait_recv(self):
-            self.each("wait_recv", True)
-
-        def wait_send(self):
-            self.each("wait_send", False)
+    def each(groups, what, incoming=False):
+        for a in (1, 2, 0):
+            for side in (0, 1):
+
+                @pl.when(exists(a, 1 - side if incoming else side))
+                def _(a=a, side=side):
+                    for group in groups:
+                        getattr(group.desc(a, side), what)()
 
     def yx_parts(ys, yh, xs, xh, at):
         return [
@@ -142,8 +138,8 @@
 
     one = pl.ds(0, 1)
     facesk = Faces(0, [
-        (kappa.at[0], kb.at[CZ + 1, rows, :]), (kappa.at[CZ - 1], kb.at[0, rows, :]),
-        *yx_parts(ysendk, yhalok, xsendk, xhalok, one),
+        (kappa.at[0], u0.at[NF, CZ + 1, rows, :]), (kappa.at[CZ - 1], u0.at[NF, 0, rows, :]),
+        *yx_parts(ysend1, yhalo1, xsend1, xhalo1, pl.ds(NF, 1)),
     ])
     faces1, faces2 = [], []
     for g, (f, n) in enumerate(GROUPS1):
@@ -171,25 +167,31 @@
 
         return lax.fori_loop(0, CZ // UNROLL, step, init)
 
-    def pack_planes(ref, ysend, xsend, f):
+    def pack_planes(f):
+        ref = u0.at[f]
+
         def body(z, q):
-            ysend[0, f, pl.ds(z, 1), :] = ref[z + 1, pl.ds(R0, 1), :]
-            ysend[1, f, pl.ds(z, 1), :] = ref[z + 1, pl.ds(R0 + CY - 1, 1), :]
+            ysend1[0, f, pl.ds(z, 1), :] = ref[z + 1, pl.ds(R0, 1), :]
+            ysend1[1, f, pl.ds(z, 1), :] = ref[z + 1, pl.ds(R0 + CY - 1, 1), :]
             for h in range(2):
                 q = packed(ref[z + 1, pl.ds(R0 + 8 * h, 8), :], q, 2 * z + h)
             return q
 
-        xsend[f] = sweep(body, blank)
+        xsend1[f] = sweep(body, blank)
 
     load_k.wait()
-    pack_planes(kb, ysendk, xsendk, 0)
-    for f in range(NF):
-        loads[f].wait()
-        pack_planes(u0.at[f], ysend1, xsend1, f)
+
+    def pack_one(i, carry):
+        @pl.when(i > 0)
+        def _():
+            load(i - 1).wait()
+
+        pack_planes(lax.rem(i + NF, NF + 1))
+        return carry
+
+    lax.fori_loop(0, NF + 1, pack_one, 0)
     pl.semaphore_wait(barrier, count)
-    facesk.start()
-    for face in faces1:
-        face.start()
+    each([facesk, *faces1], "start")
     greet(token.at[0])
 
     def sides(ref, z, h, yhalo, f, pack):
@@ -206,13 +208,13 @@
         xp = jnp.where(last_lane, edge, rolled(mid, CX - 1))
         return mid, zm, zp, ym, yp, xm, xp
 
-    facesk.wait_recv()
-    kpack = halo_pack(xhalok, 0)
+    each([facesk], "wait_recv", True)
+    kpack = halo_pack(xhalo1, NF)
 
     def coefficients(z, carry):
         for h in range(2):
             at = pl.ds(8 * h, 8)
-            mid, *others = sides(kb, z, h, yhalok, 0, kpack)
+            mid, *others = sides(u0.at[NF], z, h, yhalo1, NF, kpack)
             means = [0.5 * (mid + w) for w in others]
             kz[z, at, :] = means[0]
             kz[z + 1, at, :] = means[1]
@@ -254,14 +256,24 @@
         xsend2[f] = sweep(advance(u0, f, yhalo1, xhalo1, emit), blank)
 
     small[0].wait()
-    arrivals1 = {f: faces1[g] for g, (f, n) in enumerate(GROUPS1)}
-    departures2 = {f + n - 1: faces2[g] for g, (f, n) in enumerate(GROUPS2)}
-    for f in range(NF):
-        if f in arrivals1:
-            arrivals1[f].wait_recv()
+
+    def first(f, carry):
+        for g, (f0, _) in enumerate(GROUPS1):
+
+            @pl.when(f == f0)
+            def _(g=g):
+                each([faces1[g]], "wait_recv", True)
+
         step1(f)
-        if f in departures2:
-            departures2[f].start()
+        for g, (f0, n) in enumerate(GROUPS2):
+
+            @pl.when(f == f0 + n - 1)
+            def _(g=g):
+                each([faces2[g]], "start")
+
+        return carry
+
+    lax.fori_loop(0, NF, first, 0)
     pl.semaphore_wait(token.at[0], 2)
     greet(token.at[1])
 
@@ -269,36 +281,41 @@
         start = h * 8 * CZ + lax.rem(z, 4) * 8 + lax.div(z, 4)
         return pl.ds(start, 8, stride=CZ)
 
-    rs2, rm2 = rs.reshape(CY * CZ, CX), rm.reshape(CY * CZ, CX)
-    rh2, rb2 = rh.reshape(CY * CZ, CX), rb.reshape(3, CY * CZ, CX)
-
-    def step2(f):
+    rs2, rh2 = rs.reshape(CY * CZ, CX), rh.reshape(CY * CZ, CX)
+    rb2 = rb.reshape(4, CY * CZ, CX)
+
+    def emit_scalar(z, h, value):
+        u2[0, z, pl.ds(8 * h, 8), :] = value
+        sp[z + 1, pl.ds(R0 + 8 * h, 8), :] = value
+        side, row = (0, 0) if h == 0 else (1, 7)
+        ysend3[side, 0, pl.ds(z, 1), :] = value[row : row + 1, :]
+        rs2[sites(z, h), :] = value
+
+    each([faces2[0]], "wait_recv", True)
+    xsend3[0] = sweep(advance(u1, 0, yhalo2, xhalo2, emit_scalar), blank)
+    each([faces3], "start")
+
+    def second(f, carry):
+        for g in (1, 2):
+
+            @pl.when(f == GROUPS2[g][0])
+            def _(g=g):
+                each([faces2[g]], "wait_recv", True)
+
+        last = f == NF - 1
+        inner = jnp.where(last, 1.0, 0.5)
+        outer = jnp.where(last, -0.5 * LOG2E, 0.5)
+        base = jnp.where(last, -LOG2E, 0.5)
+
         def emit(z, h, value):
-            at = pl.ds(8 * h, 8)
-            u2[f, z, at, :] = value
-            if f == 0:
-                sp[z + 1, pl.ds(R0 + 8 * h, 8), :] = value
-                side, row = (0, 0) if h == 0 else (1, 7)
-                ysend3[side, 0, pl.ds(z, 1), :] = value[row : row + 1, :]
-                rs2[sites(z, h), :] = value
-            elif f == 4:
-                rm2[sites(z, h), :] = (-LOG2E) - (0.5 * LOG2E) * jnp.tanh(value)
-            else:
-                rb2[f - 1, sites(z, h), :] = 0.5 + 0.5 * jnp.tanh(0.5 * value)
-
-        out = sweep(advance(u1, f, yhalo2, xhalo2, emit), blank if f == 0 else None)
-        if f == 0:
-            xsend3[0] = out
-
-    arrivals2 = {f: faces2[g] for g, (f, n) in enumerate(GROUPS2)}
-    for f in range(NF):
-        if f in arrivals2:
-            arrivals2[f].wait_recv()
-        step2(f)
-        if f == 0:
-            faces3.start()
-
-    faces3.wait_recv()
+            u2[f, z, pl.ds(8 * h, 8), :] = value
+            rb2[f - 1, sites(z, h), :] = base + outer * jnp.tanh(inner * value)
+
+        sweep(advance(u1, f, yhalo2, xhalo2, emit), None)
+        return carry
+
+    lax.fori_loop(1, NF, second, 0)
+    each([faces3], "wait_recv", True)
     spack = halo_pack(xhalo3, 0)
 
     def shading(z, carry):
@@ -357,7 +374,7 @@
                 cover = mask[0, t, 0, y].astype(f32)
                 mid, slope, amount = center[t], -LOG2E * sharp[t], gain[t]
                 gap = rs[y] - mid
-                depth = jnp.exp2(slope * (gap * gap)) * (amount * rm[y])
+                depth = jnp.exp2(slope * (gap * gap)) * (amount * rb[3, y])
                 e = [depth[0:8]]
                 for w in range(1, 4):
                     e.append(e[-1] + depth[8 * w : 8 * w + 8])
@@ -383,8 +400,8 @@
         lax.fori_loop(0, per_owner // 8, eight, 0)
 
     def merge(theirs, own):
-        for i in range(per_owner // 8):
-            at = pl.ds(8 * i, 8)
+        def part(i, carry):
+            at = pl.ds(pl.multiple_of(8 * i, 8), 8)
             a = [theirs[k, at, :] for k in range(4)]
             b = [own[k, at, :] for k in range(4)]
             front = [jnp.where(odd == 1, x, y) for x, y in zip(a, b)]
@@ -392,63 +409,73 @@
             clear = 1.0 - front[3]
             for k in range(4):
                 own[k, at, :] = front[k] + clear * back[k]
-
-    def to_mate(d):
-        return block_copy(pairs + d, mtiles.at[d - 1], mrecv.at[d - 1], mate)
-
-    def onward(d):
+            return carry
+
+        lax.fori_loop(0, per_owner // 8, part, 0)
+
+    def to_mate(k):
+        return block_copy(pairs + 1 + k, blocks.at[k], mrecv.at[k], mate)
+
+    def onward(k):
         return pltpu.make_async_remote_copy(
-            src_ref=rtiles.at[d - 1], dst_ref=recv.at[mine],
-            send_sem=tile_send.at[d - 1], recv_sem=tile_recv.at[mine],
-            device_id={"gz": at_distance(mes[0], d)}, device_id_type=MESH,
+            src_ref=blocks.at[relays + k], dst_ref=recv.at[mine],
+            send_sem=tile_send.at[k], recv_sem=tile_recv.at[mine],
+            device_id={"gz": at_distance(mes[0], relays - k)}, device_id_type=MESH,
         )
 
-    def pass_on(d):
-        to_mate(d).wait_recv()
-        merge(mrecv.at[d - 1], rtiles.at[d - 1])
-        onward(d).start()
-
-    order = list(range(relays, 0, -1))
-    for d in order:
-        render(at_distance(mate, -d), mtiles.at[d - 1])
-        to_mate(d).start()
-    pair_copy = block_copy(pairs, ptiles, precv, mate)
-    for j, d in enumerate(order):
-        render(at_distance(mes[0], d), rtiles.at[d - 1])
-        if j:
-            pass_on(order[j - 1])
-    render(mate, ptiles)
-    pair_copy.start()
-    if order:
-        pass_on(order[-1])
-    render(mes[0], recv.at[mine])
+    pair_copy = block_copy(pairs, blocks.at[2 * relays], precv, mate)
+
+    def owner_step(k, carry):
+        off = jnp.where(k < relays, k - relays - 1, jnp.where(k < 2 * relays, 2 * relays - k, k - 2 * relays - 1))
+        render(at_distance(mes[0], off), blocks.at[k])
+
+        @pl.when(k < relays)
+        def _():
+            to_mate(k).start()
+
+        @pl.when(k == 2 * relays)
+        def _():
+            pair_copy.start()
+
+        @pl.when(jnp.logical_and(k > relays, k <= 2 * relays))
+        def _():
+            r = k - relays - 1
+            to_mate(r).wait_recv()
+            merge(mrecv.at[r], blocks.at[relays + r])
+            onward(r).start()
+
+        return carry
+
+    lax.fori_loop(0, nz, owner_step, 0)
     pair_copy.wait_recv()
-    merge(precv, recv.at[mine])
+    merge(precv, blocks.at[nz - 1])
     for o in range(1, pairs):
         q = lax.rem(mine + o, pairs)
         pltpu.make_async_remote_copy(
-            src_ref=rtiles.at[0], dst_ref=recv.at[q], send_sem=tile_send.at[0], recv_sem=tile_recv.at[q],
+            src_ref=blocks.at[0], dst_ref=recv.at[q], send_sem=tile_send.at[0], recv_sem=tile_recv.at[q],
             device_id={"gz": mate}, device_id_type=MESH,
         ).wait_recv()
 
+    def block_of(s, k, at):
+        return jnp.where(mine == s, blocks[nz - 1, k, at, :], recv[s, k, at, :])
+
     def composite(i, carry):
         at = pl.ds(pl.multiple_of(8 * i, 8), 8)
-        acc = [recv[0, k, at, :] for k in range(4)]
+        acc = [block_of(0, k, at) for k in range(4)]
         for s in range(1, pairs):
             clear = 1.0 - acc[3]
-            acc = [acc[k] + clear * recv[s, k, at, :] for k in range(4)]
+            acc = [acc[k] + clear * block_of(s, k, at) for k in range(4)]
         for k in range(4):
             for r in range(8):
                 pic_out[0, 0, 8 * i + r, pl.ds(k, 1), :] = acc[k][r : r + 1, :]
         return carry
 
     lax.fori_loop(0, per_owner // 8, composite, 0)
-    for d in order:
-        to_mate(d).wait_send()
-        onward(d).wait_send()
+    for k in range(relays):
+        to_mate(k).wait_send()
+        onward(k).wait_send()
     pair_copy.wait_send()
-    for face in [facesk, *faces1, *faces2, faces3]:
-        face.wait_send()
+    each([facesk, *faces1, *faces2, faces3], "wait_send")
 
 
 def flush(state, picture, state_out, picture_out, sem):
@@ -482,19 +509,18 @@
         in_specs=[anywhere] * 9,
         out_specs=(inside, inside),
         scratch_shapes=[
-            vm((CZ + 2, 32, CX), f32),
-            vm((NF, CZ + 2, 32, CX), f32),
+            vm((NF + 1, CZ + 2, 32, CX), f32),
             vm((NF, CZ + 2, 32, CX), f32),
             vm((CZ + 2, 32, CX), f32),
-            *halo(1), *halo(NF), *halo(NF), *halo(1),
+            *halo(NF + 1), *halo(NF), *halo(1),
             vm((CZ + 1, CY, CX), f32),
             vm((5, CZ, CY, CX), f32),
             vm((CY, CZ, CX), f32),
             vm((CY, CZ, CX), f32),
-            vm((CY, CZ, CX), f32),
-            vm((3, CY, CZ, CX), f32),
-            *[vm((max(nz // 2 - 1, 1), 4, per_owner, CX), f32)] * 3,
-            *[vm((4, per_owner, CX), f32)] * 2,
+            vm((4, CY, CZ, CX), f32),
+            vm((nz, 4, per_owner, CX), f32),
+            vm((max(nz // 2 - 1, 1), 4, per_owner, CX), f32),
+            vm((4, per_owner, CX), f32),
             vm((nz // 2, 4, per_owner, CX), f32),
             *[sm(a) for a in operands[2:]],
             pltpu.SemaphoreType.DMA((42,)),

time: 39.4 us -> 35 us (0.89)
  Pallas kernels: 38.5 us -> 33.7 us
    pallas_call x1, Pallas kernels: 37.4 us -> 32.6 us  [shards(): pl.pallas_call(kernel, out_shape=(vm((NF, CZ, CY, CX), f32), vm((1, 1, pe...]
where the time goes in v5:
time: 35 us; the launch traced here: 34.4 us
  Pallas kernels  33.7 us (96%)
  between operations  0.64 us (2%)
    pallas_call x1, Pallas kernels, shards(): pl.pallas_call(kernel, out_shape=(vm((NF, CZ, CY, CX), f32), vm((1, 1, pe...  32.6 us
    pallas_call x1, Pallas kernels, shards(): pl.pallas_call(flush, out_shape=tuple((jax.ShapeDtypeStruct(r.shape, f32)...  1.12 us

profile of v5, /device:TPU:1, one launch (start us, length us, event | category | flops | bytes accessed | tf_op | source)
XLA Modules:
  0.0 34.4 jit_solution(12969678522254298982)
XLA Ops:
  0.6 32.6 %insitu.1 = (f32[5,32,16,128]{3,2,1,0:T(8,128)S(1)}, f32[1,1,32,4,128]{4,3,2,1,0:T(4,128)S(1)}) custom-call(f32[5,32,16,128]{3,2,1,0:T(8,128)} %fields.1, f32[32,16,128]{2,1,0:T(8,128)} %kappa.1, f32[3,5]{1,0:T(4,128)} %bitcast.3, f32[16]{0:T(128)} %center_in.1, f32[16]{0:T(128)} %sharp_in.1, f32[16]{0:T(128)} %gain_in.1, f32[3,16]{1,0:T(4,128)} %color_in.1, ...), custom_call_target="tpu_custom_call" | custom-call | tf_op jit(solution)/shard_map/insitu/pallas_call | solution.py:506
  33.2 1.1 %flush.1 = (f32[5,32,16,128]{3,2,1,0:T(8,128)}, f32[1,1,32,4,128]{4,3,2,1,0:T(4,128)}) custom-call(f32[5,32,16,128]{3,2,1,0:T(8,128)S(1)} %get-tuple-element.4.state, f32[1,1,32,4,128]{4,3,2,1,0:T(4,128)S(1)} %get-tuple-element.5.picture), custom_call_target="tpu_custom_call" | custom-call | tf_op jit(solution)/shard_map/flush/pallas_call | solution.py:536

commit v6 on v5

--- a/solution.py
+++ b/solution.py
@@ -90,6 +90,9 @@
 
     def rolled(x, shift):
         return pltpu.roll(x, shift, 1)
+
+    def wrap(shift):
+        return shift % 128 if isinstance(shift, int) else lax.rem(shift, 128)
 
     def packed(value, into, v):
         return jnp.where(pair == v, rolled(value, 2 * v), into)
@@ -159,13 +162,15 @@
         *yx_parts(ysend3, yhalo3, xsend3, xhalo3, one),
     ])
 
-    def sweep(body, init):
+    def sweep(body, init, unroll=CZ):
         def step(i, carry):
-            for j in range(UNROLL):
-                carry = body(UNROLL * i + j, carry)
+            for j in range(unroll):
+                carry = body(unroll * i + j, carry)
             return carry
 
-        return lax.fori_loop(0, CZ // UNROLL, step, init)
+        if unroll == CZ:
+            return step(0, init)
+        return lax.fori_loop(0, CZ // unroll, step, init)
 
     def pack_planes(f):
         ref = u0.at[f]
@@ -187,11 +192,21 @@
             load(i - 1).wait()
 
         pack_planes(lax.rem(i + NF, NF + 1))
+
+        @pl.when(i == 0)
+        def _():
+            pl.semaphore_wait(barrier, count)
+            each([facesk], "start")
+
+        for g, (f0, n) in enumerate(GROUPS1):
+
+            @pl.when(i == f0 + n)
+            def _(g=g):
+                each([faces1[g]], "start")
+
         return carry
 
     lax.fori_loop(0, NF + 1, pack_one, 0)
-    pl.semaphore_wait(barrier, count)
-    each([facesk, *faces1], "start")
     greet(token.at[0])
 
     def sides(ref, z, h, yhalo, f, pack):
@@ -203,7 +218,7 @@
             ym = jnp.where(first_row, jnp.broadcast_to(yhalo[0, f, pl.ds(z, 1), :], (8, 128)), ym)
         else:
             yp = jnp.where(last_row, jnp.broadcast_to(yhalo[1, f, pl.ds(z, 1), :], (8, 128)), yp)
-        edge = rolled(pack, lax.rem(128 - 2 * (2 * z + h), 128))
+        edge = rolled(pack, wrap(128 - 2 * (2 * z + h)))
         xm = jnp.where(first_lane, edge, rolled(mid, 1))
         xp = jnp.where(last_lane, edge, rolled(mid, CX - 1))
         return mid, zm, zp, ym, yp, xm, xp
@@ -223,7 +238,7 @@
             kf[4, z, at, :] = 1.0 - ((means[0] + means[1]) + (means[2] + means[3]) + (means[4] + means[5]))
         return carry
 
-    sweep(coefficients, 0)
+    sweep(coefficients, 0, UNROLL)
 
     def advance(src, f, yhalo, xhalo, emit):
         pack = halo_pack(xhalo, f)
@@ -278,7 +293,7 @@
     greet(token.at[1])
 
     def sites(z, h):
-        start = h * 8 * CZ + lax.rem(z, 4) * 8 + lax.div(z, 4)
+        start = h * 8 * CZ + z % 4 * 8 + z // 4 if isinstance(z, int) else h * 8 * CZ + lax.rem(z, 4) * 8 + lax.div(z, 4)
         return pl.ds(start, 8, stride=CZ)
 
     rs2, rh2 = rs.reshape(CY * CZ, CX), rh.reshape(CY * CZ, CX)
@@ -292,7 +307,7 @@
         rs2[sites(z, h), :] = value
 
     each([faces2[0]], "wait_recv", True)
-    xsend3[0] = sweep(advance(u1, 0, yhalo2, xhalo2, emit_scalar), blank)
+    xsend3[0] = sweep(advance(u1, 0, yhalo2, xhalo2, emit_scalar), blank, UNROLL)
     each([faces3], "start")
 
     def second(f, carry):
@@ -328,7 +343,7 @@
             rh2[sites(z, h), :] = shade
         return carry
 
-    sweep(shading, 0)
+    sweep(shading, 0, UNROLL)
     for copy in small[1:]:
         copy.wait()
     pl.semaphore_wait(token.at[1], 2)
@@ -348,56 +363,37 @@
             device_id={"gz": z}, device_id_type=MESH,
         )
 
-    def gather_rows(x):
-        low, mid, bit = sub < 4, lax.bitwise_and(sub, 2) == 0, lax.bitwise_and(sub, 1) == 0
-        x = [
-            jnp.where(low, x[i], x[i + 4]) + pltpu.roll(jnp.where(low, x[i + 4], x[i]), 4, 0)
-            for i in range(4)
-        ]
-        for mask_, step in ((mid, 2), (bit, 1)):
-            x = [
-                jnp.where(
-                    mask_, x[i] + pltpu.roll(x[i], 8 - step, 0), x[i + step] + pltpu.roll(x[i + step], step, 0)
-                )
-                for i in range(step)
-            ]
-        return x[0]
-
     def render(owner, dst):
-        def eight(i8, carry):
-            sums = [[], [], []]
-            for j in range(8):
-                i = 8 * i8 + j
-                p = perm[0, 0, owner * per_owner + i]
-                t = lax.shift_right_logical(p, 4)
-                y = lax.bitwise_and(p, 15)
-                cover = mask[0, t, 0, y].astype(f32)
-                mid, slope, amount = center[t], -LOG2E * sharp[t], gain[t]
-                gap = rs[y] - mid
-                depth = jnp.exp2(slope * (gap * gap)) * (amount * rb[3, y])
-                e = [depth[0:8]]
+        def tile(i, carry):
+            p = perm[0, 0, owner * per_owner + i]
+            t = lax.shift_right_logical(p, 4)
+            y = lax.bitwise_and(p, 15)
+            cover = mask[0, t, 0, y].astype(f32)
+            mid, slope, amount = center[t], -LOG2E * sharp[t], gain[t]
+            gap = rs[y] - mid
+            depth = jnp.exp2(slope * (gap * gap)) * (amount * rb[3, y])
+            e = [depth[0:8]]
+            for w in range(1, 4):
+                e.append(e[-1] + depth[8 * w : 8 * w + 8])
+            inclusive = e[3]
+            for sh in (1, 2, 4):
+                inclusive = inclusive + jnp.where(sub >= sh, pltpu.roll(inclusive, sh, 0), 0.0)
+            before = jnp.exp2(inclusive - e[3])
+            lit = [jnp.exp2(x) for x in e]
+            weight = [1.0 - lit[0]] + [lit[w] - lit[w + 1] for w in range(3)]
+            shade = rh[y]
+            weight = [weight[w] * shade[8 * w : 8 * w + 8] for w in range(4)]
+            for k in range(3):
+                base = rb[k, y]
+                total = weight[0] * base[0:8]
                 for w in range(1, 4):
-                    e.append(e[-1] + depth[8 * w : 8 * w + 8])
-                inclusive = e[3]
-                for sh in (1, 2, 4):
-                    inclusive = inclusive + jnp.where(sub >= sh, pltpu.roll(inclusive, sh, 0), 0.0)
-                before = jnp.exp2(inclusive - e[3])
-                lit = [jnp.exp2(x) for x in e]
-                weight = [1.0 - lit[0]] + [lit[w] - lit[w + 1] for w in range(3)]
-                shade = rh[y]
-                weight = [weight[w] * shade[8 * w : 8 * w + 8] for w in range(4)]
-                for k in range(3):
-                    base = rb[k, y]
-                    total = weight[0] * base[0:8]
-                    for w in range(1, 4):
-                        total = total + weight[w] * base[8 * w : 8 * w + 8]
-                    sums[k].append((total * before) * (color[k, t] * cover))
-                dst[3, pl.ds(i, 1), :] = (1.0 - jnp.exp2(inclusive[7:8])) * cover
-            for k in range(3):
-                dst[k, pl.ds(pl.multiple_of(8 * i8, 8), 8), :] = gather_rows(sums[k])
+                    total = total + weight[w] * base[8 * w : 8 * w + 8]
+                total = jnp.sum(total * before, axis=0, keepdims=True)
+                dst[k, pl.ds(i, 1), :] = total * (color[k, t] * cover)
+            dst[3, pl.ds(i, 1), :] = (1.0 - jnp.exp2(inclusive[7:8])) * cover
             return carry
 
-        lax.fori_loop(0, per_owner // 8, eight, 0)
+        lax.fori_loop(0, per_owner, tile, 0, unroll=8)
 
     def merge(theirs, own):
         def part(i, carry):

time: 35 us -> 35.5 us (1.014); the launches traced: 34.4 us -> 35.3 us
  Pallas kernels: 33.7 us -> 34.6 us
    pallas_call x1, Pallas kernels: 32.6 us -> 33.5 us  [shards(): pl.pallas_call(kernel, out_shape=(vm((NF, CZ, CY, CX), f32), vm((1, 1, pe...]
where the time goes in v6:
time: 35.5 us; the launch traced here: 35.3 us
  Pallas kernels  34.6 us (97%)
  between operations  0.64 us (2%)
    pallas_call x1, Pallas kernels, shards(): pl.pallas_call(kernel, out_shape=(vm((NF, CZ, CY, CX), f32), vm((1, 1, pe...  33.5 us
    pallas_call x1, Pallas kernels, shards(): pl.pallas_call(flush, out_shape=tuple((jax.ShapeDtypeStruct(r.shape, f32)...  1.12 us

profile of v6, /device:TPU:1, one launch (start us, length us, event | category | flops | bytes accessed | tf_op | source)
XLA Modules:
  0.0 35.3 jit_solution(3057735006545691179)
XLA Ops:
  0.6 33.5 %insitu.1 = (f32[5,32,16,128]{3,2,1,0:T(8,128)S(1)}, f32[1,1,32,4,128]{4,3,2,1,0:T(4,128)S(1)}) custom-call(f32[5,32,16,128]{3,2,1,0:T(8,128)} %fields.1, f32[32,16,128]{2,1,0:T(8,128)} %kappa.1, f32[3,5]{1,0:T(4,128)} %bitcast.3, f32[16]{0:T(128)} %center_in.1, f32[16]{0:T(128)} %sharp_in.1, f32[16]{0:T(128)} %gain_in.1, f32[3,16]{1,0:T(4,128)} %color_in.1, ...), custom_call_target="tpu_custom_call" | custom-call | tf_op jit(solution)/shard_map/insitu/pallas_call | solution.py:502
  34.1 1.1 %flush.1 = (f32[5,32,16,128]{3,2,1,0:T(8,128)}, f32[1,1,32,4,128]{4,3,2,1,0:T(4,128)}) custom-call(f32[5,32,16,128]{3,2,1,0:T(8,128)S(1)} %get-tuple-element.4.state, f32[1,1,32,4,128]{4,3,2,1,0:T(4,128)S(1)} %get-tuple-element.5.picture), custom_call_target="tpu_custom_call" | custom-call | tf_op jit(solution)/shard_map/flush/pallas_call | solution.py:532

commit v7 on v3

--- a/solution.py
+++ b/solution.py
@@ -13,8 +13,8 @@
 NF, CZ, CY, CX, TF = 5, 32, 16, 128, 16
 R0 = 8
 TILES = TF * CY
-GROUPS1 = ((0, 2), (2, 3))
-GROUPS2 = ((0, 1), (1, 2), (3, 2))
+GROUPS1 = ((0, 1), (1, 1), (2, 1), (3, 1), (4, 1))
+GROUPS2 = ((0, 1), (1, 1), (2, 1), (3, 1), (4, 1))
 UNROLL = 16
 
 
@@ -154,11 +154,11 @@
         ]))
     for g, (f, n) in enumerate(GROUPS2):
         at = pl.ds(f, n)
-        faces2.append(Faces(18 + 6 * g, [
+        faces2.append(Faces(36 + 6 * g, [
             (u1.at[at, 1, rows, :], u1.at[at, CZ + 1, rows, :]), (u1.at[at, CZ, rows, :], u1.at[at, 0, rows, :]),
             *yx_parts(ysend2, yhalo2, xsend2, xhalo2, at),
         ]))
-    faces3 = Faces(36, [
+    faces3 = Faces(66, [
         (sp.at[1, rows, :], sp.at[CZ + 1, rows, :]), (sp.at[CZ, rows, :], sp.at[0, rows, :]),
         *yx_parts(ysend3, yhalo3, xsend3, xhalo3, one),
     ])
@@ -183,15 +183,16 @@
 
     load_k.wait()
     pack_planes(kb, ysendk, xsendk, 0)
+    pl.semaphore_wait(barrier, count)
+    facesk.start()
     for f in range(NF):
         loads[f].wait()
         pack_planes(u0.at[f], ysend1, xsend1, f)
+        for g, (f0, n) in enumerate(GROUPS1):
+            if f == f0 + n - 1:
+                faces1[g].start()
     for copy in small:
         copy.wait()
-    pl.semaphore_wait(barrier, count)
-    facesk.start()
-    for face in faces1:
-        face.start()
     greet(token.at[0])
 
     def sides(ref, z, h, yhalo, f, pack):
@@ -360,7 +361,7 @@
             dst[3, pl.ds(i, 1), :] = (1.0 - jnp.exp2(inclusive[7:8])) * cover
             return carry
 
-        lax.fori_loop(0, per_owner, tile, 0, unroll=8)
+        lax.fori_loop(0, per_owner, tile, 0, unroll=4)
 
     def merge(theirs, own):
         for i in range(per_owner // 8):
@@ -477,8 +478,8 @@
             *[vm((4, per_owner, CX), f32)] * 2,
             vm((nz // 2, 4, per_owner, CX), f32),
             *[sm(a) for a in operands[2:]],
-            pltpu.SemaphoreType.DMA((42,)),
-            pltpu.SemaphoreType.DMA((42,)),
+            pltpu.SemaphoreType.DMA((72,)),
+            pltpu.SemaphoreType.DMA((72,)),
             pltpu.SemaphoreType.DMA((nz,)),
             pltpu.SemaphoreType.DMA((nz,)),
             pltpu.SemaphoreType.DMA((13,)),

time: 34.2 us -> 33.6 us (0.982)
  Pallas kernels: 33.5 us -> 32.7 us
    pallas_call x1, Pallas kernels: 32.3 us -> 31.6 us  [shards(): pl.pallas_call(kernel, out_shape=(vm((NF, CZ, CY, CX), f32), vm((1, 1, pe...]
where the time goes in v7:
time: 33.6 us; the launch traced here: 33.4 us
  Pallas kernels  32.7 us (97%)
  between operations  0.64 us (2%)
    pallas_call x1, Pallas kernels, shards(): pl.pallas_call(kernel, out_shape=(vm((NF, CZ, CY, CX), f32), vm((1, 1, pe...  31.6 us
    pallas_call x1, Pallas kernels, shards(): pl.pallas_call(flush, out_shape=tuple((jax.ShapeDtypeStruct(r.shape, f32)...  1.12 us

profile of v7, /device:TPU:1, one launch (start us, length us, event | category | flops | bytes accessed | tf_op | source)
XLA Modules:
  0.0 33.4 jit_solution(6947147634893121251)
XLA Ops:
  0.6 31.6 %insitu.1 = (f32[5,32,16,128]{3,2,1,0:T(8,128)S(1)}, f32[1,1,32,4,128]{4,3,2,1,0:T(4,128)S(1)}) custom-call(f32[5,32,16,128]{3,2,1,0:T(8,128)} %fields.1, f32[32,16,128]{2,1,0:T(8,128)} %kappa.1, f32[3,5]{1,0:T(4,128)} %bitcast.3, f32[16]{0:T(128)} %center_in.1, f32[16]{0:T(128)} %sharp_in.1, f32[16]{0:T(128)} %gain_in.1, f32[3,16]{1,0:T(4,128)} %color_in.1, ...), custom_call_target="tpu_custom_call" | custom-call | tf_op jit(solution)/shard_map/insitu/pallas_call | solution.py:460
  32.3 1.1 %flush.1 = (f32[5,32,16,128]{3,2,1,0:T(8,128)}, f32[1,1,32,4,128]{4,3,2,1,0:T(4,128)}) custom-call(f32[5,32,16,128]{3,2,1,0:T(8,128)S(1)} %get-tuple-element.4.state, f32[1,1,32,4,128]{4,3,2,1,0:T(4,128)S(1)} %get-tuple-element.5.picture), custom_call_target="tpu_custom_call" | custom-call | tf_op jit(solution)/shard_map/flush/pallas_call | solution.py:491

commit v8 on v7

--- a/solution.py
+++ b/solution.py
@@ -35,6 +35,30 @@
     per_owner = TILES // nz
     rows = pl.ds(R0, CY)
 
+    def exists(a, side):
+        return (mes[a] > 0) if side == 0 else (mes[a] < sizes[a] - 1)
+
+    ring = [lax.rem(mes[0] + 1, nz), lax.rem(mes[0] + nz - 1, nz)]
+    barrier = pltpu.get_barrier_semaphore()
+
+    def greet(sem):
+        for z in ring:
+            pl.semaphore_signal(sem, inc=1, device_id={"gz": z}, device_id_type=MESH)
+
+    greet(barrier)
+    count = jnp.int32(2)
+    for a in (1, 2):
+        for side in (0, 1):
+            ok = exists(a, side)
+
+            @pl.when(ok)
+            def _(a=a, side=side):
+                pl.semaphore_signal(
+                    barrier, inc=1, device_id={names[a]: mes[a] + 2 * side - 1}, device_id_type=MESH
+                )
+
+            count = count + ok.astype(jnp.int32)
+
     def local(i, src, dst):
         copy = pltpu.make_async_copy(src, dst, local_sem.at[i])
         copy.start()
@@ -51,30 +75,6 @@
             )
         )
     ]
-
-    def exists(a, side):
-        return (mes[a] > 0) if side == 0 else (mes[a] < sizes[a] - 1)
-
-    ring = [lax.rem(mes[0] + 1, nz), lax.rem(mes[0] + nz - 1, nz)]
-    barrier = pltpu.get_barrier_semaphore()
-
-    def greet(sem):
-        for z in ring:
-            pl.semaphore_signal(sem, inc=1, device_id={"gz": z}, device_id_type=MESH)
-
-    greet(barrier)
-    count = jnp.int32(2)
-    for a in (1, 2):
-        for side in (0, 1):
-            ok = exists(a, side)
-
-            @pl.when(ok)
-            def _(a=a, side=side):
-                pl.semaphore_signal(
-                    barrier, inc=1, device_id={names[a]: mes[a] + 2 * side - 1}, device_id_type=MESH
-                )
-
-            count = count + ok.astype(jnp.int32)
 
     lane = lax.broadcasted_iota(jnp.int32, (8, 128), 1)
     sub = lax.broadcasted_iota(jnp.int32, (8, 128), 0)

time: 33.6 us -> 33.5 us (level)
  no operation moved by 1% of the time
where the time goes in v8:
time: 33.5 us; the launch traced here: 33.3 us
  Pallas kernels  32.7 us (98%)
  between operations  0.64 us (2%)
    pallas_call x1, Pallas kernels, shards(): pl.pallas_call(kernel, out_shape=(vm((NF, CZ, CY, CX), f32), vm((1, 1, pe...  31.6 us
    pallas_call x1, Pallas kernels, shards(): pl.pallas_call(flush, out_shape=tuple((jax.ShapeDtypeStruct(r.shape, f32)...  1.12 us

profile of v8, /device:TPU:1, one launch (start us, length us, event | category | flops | bytes accessed | tf_op | source)
XLA Modules:
  0.0 33.3 jit_solution(9787219316578144274)
XLA Ops:
  0.6 31.6 %insitu.1 = (f32[5,32,16,128]{3,2,1,0:T(8,128)S(1)}, f32[1,1,32,4,128]{4,3,2,1,0:T(4,128)S(1)}) custom-call(f32[5,32,16,128]{3,2,1,0:T(8,128)} %fields.1, f32[32,16,128]{2,1,0:T(8,128)} %kappa.1, f32[3,5]{1,0:T(4,128)} %bitcast.3, f32[16]{0:T(128)} %center_in.1, f32[16]{0:T(128)} %sharp_in.1, f32[16]{0:T(128)} %gain_in.1, f32[3,16]{1,0:T(4,128)} %color_in.1, ...), custom_call_target="tpu_custom_call" | custom-call | tf_op jit(solution)/shard_map/insitu/pallas_call | solution.py:460
  32.2 1.1 %flush.1 = (f32[5,32,16,128]{3,2,1,0:T(8,128)}, f32[1,1,32,4,128]{4,3,2,1,0:T(4,128)}) custom-call(f32[5,32,16,128]{3,2,1,0:T(8,128)S(1)} %get-tuple-element.4.state, f32[1,1,32,4,128]{4,3,2,1,0:T(4,128)S(1)} %get-tuple-element.5.picture), custom_call_target="tpu_custom_call" | custom-call | tf_op jit(solution)/shard_map/flush/pallas_call | solution.py:491
